TPU v7x, 32 devices: a whole 2x2x4 slice. The times are simulated.
32 devices in a mesh: gx: 4 (over x, core), gy: 2 (over y), gz: 4 (over z).
Axes of the slice: x: 2, y: 2, z: 4, core: 2. Of those that a mesh axis runs over, the one named last changes fastest.
Arguments:
- coarse_pdfs: float32 [19, 16, 8, 256], P(None, 'gx', 'gy', 'gz'), may hold values from 0.1 to 32
- fine_pdfs: float32 [19, 16, 16, 512], P(None, 'gx', 'gy', 'gz'), may hold values from 0.1 to 32
- centers: int32 [3, 3, 1, 1, 8], replicated, may hold values from 4 to 59, as said below
- sphere_velocity: float32 [3, 1, 1, 8], replicated, may hold values from -0.05 to 0.05
Outputs:
- coarse_next: float32 [19, 16, 8, 256], P(None, 'gx', 'gy', 'gz')
- fine_next: float32 [19, 16, 16, 512], P(None, 'gx', 'gy', 'gz')
- sphere_force: float32 [2, 3, 1, 1, 8], replicated
Inputs may be any that keep to these rules, and one draw needn't show every extreme that they name: `centers`: each coordinate of a center is counted from its box's first cell; from one substep to the next it changes by -1, 0 or 1, and the same change repeats in the second substep.
All inputs are finite; a program needn't handle non-finite values.
Results may differ from a plain program's by a relative error of at most 0.0003.
Values sent between devices are 32-bit elements; how exact they have to be, the bound alone decides.
A program may use at most 64 MiB of HBM per device.

v0:
```python
import jax
import jax.numpy as jnp
from jax import lax
from jax.sharding import PartitionSpec as P

BOX_XY = 16
BOX_Z = 64
RADIUS = 4


VELOCITIES = (
    (0, 0, 0),
    (1, 0, 0),
    (-1, 0, 0),
    (0, 1, 0),
    (0, -1, 0),
    (0, 0, 1),
    (0, 0, -1),
    (1, 1, 0),
    (-1, -1, 0),
    (1, -1, 0),
    (-1, 1, 0),
    (1, 0, 1),
    (-1, 0, -1),
    (1, 0, -1),
    (-1, 0, 1),
    (0, 1, 1),
    (0, -1, -1),
    (0, 1, -1),
    (0, -1, 1),
)
OPPOSITE = (0, 2, 1, 4, 3, 6, 5, 8, 7, 10, 9, 12, 11, 14, 13, 16, 15, 18, 17)
WEIGHTS = (1.0 / 3.0,) + (1.0 / 18.0,) * 6 + (1.0 / 36.0,) * 12
COARSE_RATE = 1.25
FINE_RATE = 1.0 / 1.1
HIGHEST = lax.Precision.HIGHEST


def extended(cells, sides, width):
    for axis, dim in sides:
        count = lax.axis_size(axis)
        head = lax.slice_in_dim(cells, 0, width, axis=dim)
        tail = lax.slice_in_dim(cells, cells.shape[dim] - width, cells.shape[dim], axis=dim)
        cells = jnp.concatenate(
            [
                lax.ppermute(tail, axis, [(i, (i + 1) % count) for i in range(count)]),
                cells,
                lax.ppermute(head, axis, [((i + 1) % count, i) for i in range(count)]),
            ],
            axis=dim,
        )
    return cells


def project(vectors, direction):
    projected = jnp.zeros_like(vectors[0])
    for dimension in range(3):
        sign = VELOCITIES[direction][dimension]
        if sign == 1:
            projected = projected + vectors[dimension]
        elif sign == -1:
            projected = projected - vectors[dimension]
    return projected


def speed_squared(vectors):
    return vectors[0] * vectors[0] + vectors[1] * vectors[1] + vectors[2] * vectors[2]


def equilibrium(density, vectors, speed_sq, direction):
    projected = project(vectors, direction)
    return (
        WEIGHTS[direction]
        * density
        * (1.0 + 3.0 * projected + 4.5 * projected * projected - 1.5 * speed_sq)
    )


def total_density(populations):
    density = populations[0]
    for direction in range(1, 19):
        density = density + populations[direction]
    return density


def collide(populations, relaxation):
    density = total_density(populations)
    velocity = []
    for dimension in range(3):
        summed = jnp.zeros_like(density)
        for direction in range(19):
            sign = VELOCITIES[direction][dimension]
            if sign == 1:
                summed = summed + populations[direction]
            elif sign == -1:
                summed = summed - populations[direction]
        velocity.append(summed / density)
    speed_sq = speed_squared(velocity)
    relaxed = []
    for direction in range(19):
        target = equilibrium(density, velocity, speed_sq, direction)
        relaxed.append(populations[direction] - relaxation * (populations[direction] - target))
    return jnp.stack(relaxed)


def box_onehot(coords, box_size, box_count):
    box_index = jnp.floor_divide(coords, box_size)
    onehot = (box_index[None, :] == jnp.arange(box_count, dtype=jnp.int32)[:, None]).astype(
        jnp.float32
    )
    offsets = (coords - box_index * box_size).astype(jnp.float32)
    return (onehot, offsets)


def geometry(coord_x, coord_y, coord_z, centers, sphere_velocity):
    count_x, count_y, count_z = (centers.shape[2], centers.shape[3], centers.shape[4])
    table_x, offset_x = box_onehot(coord_x, BOX_XY, count_x)
    table_y, offset_y = box_onehot(coord_y, BOX_XY, count_y)
    table_z, offset_z = box_onehot(coord_z, BOX_Z, count_z)
    inside = ((coord_x >= 0) & (coord_x < count_x * BOX_XY))[:, None, None]

    def spread(values):
        return jnp.einsum("abc,ax,by,cz->xyz", values, table_x, table_y, table_z, precision=HIGHEST)

    solids = []
    for moment in range(3):
        gap_x = offset_x[:, None, None] - spread(centers[moment, 0].astype(jnp.float32))
        gap_y = offset_y[None, :, None] - spread(centers[moment, 1].astype(jnp.float32))
        gap_z = offset_z[None, None, :] - spread(centers[moment, 2].astype(jnp.float32))
        distance = gap_x * gap_x + gap_y * gap_y + gap_z * gap_z
        solids.append((distance <= float(RADIUS * RADIUS)) & inside)
    velocity_field = [spread(sphere_velocity[dimension]) for dimension in range(3)]
    return (solids, velocity_field, (table_x, table_y, table_z))


def pull_from(values, direction):
    step_x, step_y, step_z = VELOCITIES[direction]
    width_x = values.shape[-3] - 2
    width_y = values.shape[-2] - 2
    width_z = values.shape[-1] - 2
    return values[
        ...,
        1 - step_x : 1 - step_x + width_x,
        1 - step_y : 1 - step_y + width_y,
        1 - step_z : 1 - step_z + width_z,
    ]


def trimmed(values, width):
    trim_by = 2 - width
    return values[..., trim_by:-trim_by, trim_by:-trim_by, trim_by:-trim_by]


def upsample(ghost_plane):
    return jnp.repeat(jnp.repeat(ghost_plane, 2, axis=1), 2, axis=2)


def coalesce(ghost_plane):
    grouped = ghost_plane.reshape(19, ghost_plane.shape[1] // 2, 2, ghost_plane.shape[2] // 2, 2)
    return (
        grouped[:, :, 0, :, 0]
        + grouped[:, :, 1, :, 0]
        + grouped[:, :, 0, :, 1]
        + grouped[:, :, 1, :, 1]
    ) * 0.25


def substep(padded, solid_prev, solid_new, velocity_field, margin, tables):
    interior = padded[:, 1:-1, 1:-1, 1:-1]
    size_x = interior.shape[1] - 2 * margin
    size_y = interior.shape[2] - 2 * margin
    size_z = interior.shape[3] - 2 * margin
    density = total_density(padded)
    density_in = density[1:-1, 1:-1, 1:-1]
    open_cells = jnp.logical_not(solid_prev) & jnp.logical_not(solid_new)
    moving = open_cells[1:-1, 1:-1, 1:-1]
    numerator = WEIGHTS[0] * density_in
    denominator = jnp.full(density_in.shape, WEIGHTS[0], jnp.float32)
    arrived = [interior[0]]
    push_sums = [
        jnp.zeros((size_x + 2, size_y + 2, size_z + 2), jnp.float32) for dimension in range(3)
    ]
    for direction in range(1, 19):
        step_x, step_y, step_z = VELOCITIES[direction]
        solid_next = pull_from(solid_new, direction)
        neighbour_velocity = [pull_from(values, direction) for values in velocity_field]
        returned = interior[OPPOSITE[direction]]
        bounced = returned + 6.0 * WEIGHTS[direction] * density_in * project(
            neighbour_velocity, direction
        )
        arrived.append(jnp.where(solid_next, bounced, pull_from(padded[direction], direction)))
        link_term = jnp.where(solid_next & moving, returned + bounced, 0.0)
        padded_term = jnp.pad(link_term, 2)
        pushed = padded_term[
            1 + step_x : 3 + step_x + size_x,
            1 + step_y : 3 + step_y + size_y,
            1 + step_z : 3 + step_z + size_z,
        ]
        for dimension in range(3):
            sign = VELOCITIES[direction][dimension]
            if sign == 1:
                push_sums[dimension] = push_sums[dimension] - pushed
            elif sign == -1:
                push_sums[dimension] = push_sums[dimension] + pushed
        open_next = pull_from(open_cells, direction).astype(jnp.float32)
        numerator = numerator + WEIGHTS[direction] * pull_from(density, direction) * open_next
        denominator = denominator + WEIGHTS[direction] * open_next
    refill_density = numerator / denominator
    own_velocity = [values[1:-1, 1:-1, 1:-1] for values in velocity_field]
    speed_sq = speed_squared(own_velocity)
    covered = solid_new[1:-1, 1:-1, 1:-1]
    uncovered = solid_prev[1:-1, 1:-1, 1:-1]
    updated = []
    for direction in range(19):
        refill = equilibrium(refill_density, own_velocity, speed_sq, direction)
        updated.append(
            jnp.where(
                covered, interior[direction], jnp.where(uncovered, refill, arrived[direction])
            )
        )
    table_x, table_y, table_z = tables
    forces = jnp.einsum(
        "kxyz,ax,by,cz->kabc", jnp.stack(push_sums), table_x, table_y, table_z, precision=HIGHEST
    )
    return (jnp.stack(updated), forces)


def reduce_forces(forces):
    return lax.psum(forces, ("gx", "gy", "gz"))


def shards(coarse_pdfs, fine_pdfs, centers, sphere_velocity):
    own_x, own_y, own_z = (fine_pdfs.shape[1], fine_pdfs.shape[2], fine_pdfs.shape[3])
    coarse_x = coarse_pdfs.shape[1]
    devices_x = lax.axis_size("gx")
    index_x = lax.axis_index("gx")
    total_x = own_x * devices_x
    total_y = own_y * lax.axis_size("gy")
    total_z = own_z * lax.axis_size("gz")
    coord_x = index_x * own_x + jnp.arange(-2, own_x + 2, dtype=jnp.int32)
    coord_y = (lax.axis_index("gy") * own_y + jnp.arange(-2, own_y + 2, dtype=jnp.int32)) % total_y
    coord_z = (lax.axis_index("gz") * own_z + jnp.arange(-2, own_z + 2, dtype=jnp.int32)) % total_z
    solids, velocity_field, tables = geometry(coord_x, coord_y, coord_z, centers, sphere_velocity)
    narrow_tables = (tables[0][:, 1:-1], tables[1][:, 1:-1], tables[2][:, 1:-1])
    narrow_velocity = [trimmed(values, 1) for values in velocity_field]
    coarse_post = collide(coarse_pdfs, COARSE_RATE)
    coarse_padded = extended(coarse_post, (("gx", 1), ("gy", 2), ("gz", 3)), 1)
    left_fill = upsample(coarse_padded[:, 0])
    right_fill = upsample(coarse_padded[:, coarse_x + 1])

    def with_explosion(fresh, width):
        trim_by = 2 - width
        span_x = coord_x.shape[0] - 2 * trim_by
        part_x = coord_x[trim_by : trim_by + span_x]
        left_part = left_fill[
            :, trim_by : left_fill.shape[1] - trim_by, trim_by : left_fill.shape[2] - trim_by
        ]
        right_part = right_fill[
            :, trim_by : right_fill.shape[1] - trim_by, trim_by : right_fill.shape[2] - trim_by
        ]
        is_left = (part_x < 0)[None, :, None, None]
        is_right = (part_x >= total_x)[None, :, None, None]
        return jnp.where(
            is_left, left_part[:, None], jnp.where(is_right, right_part[:, None], fresh)
        )

    first_post = extended(collide(fine_pdfs, FINE_RATE), (("gx", 1), ("gy", 2), ("gz", 3)), 2)
    middle, first_forces = substep(
        with_explosion(first_post[:, 1:-1, 1:-1, 1:-1], 1),
        trimmed(solids[0], 1),
        trimmed(solids[1], 1),
        narrow_velocity,
        0,
        narrow_tables,
    )
    second_post = extended(collide(middle, FINE_RATE), (("gx", 1), ("gy", 2), ("gz", 3)), 1)
    second_padded = with_explosion(second_post, 1)
    fine_next, second_forces = substep(
        second_padded,
        trimmed(solids[1], 1),
        trimmed(solids[2], 1),
        narrow_velocity,
        0,
        narrow_tables,
    )
    left_coal = coalesce(first_post[:, 1])
    right_coal = coalesce(first_post[:, own_x + 2])
    ghost_x = jnp.arange(coarse_x + 2, dtype=jnp.int32)
    left_ghost = ((ghost_x == 0) & (index_x == 0))[None, :, None, None]
    right_ghost = ((ghost_x == coarse_x + 1) & (index_x == devices_x - 1))[None, :, None, None]
    coarse_ready = jnp.where(
        left_ghost, left_coal[:, None], jnp.where(right_ghost, right_coal[:, None], coarse_padded)
    )
    coarse_next = jnp.stack(
        [pull_from(coarse_ready[direction], direction) for direction in range(19)]
    )
    sphere_force = jnp.stack([reduce_forces(first_forces), reduce_forces(second_forces)])
    return (coarse_next, fine_next, sphere_force)


def solution(mesh):
    in_specs = (P(None, "gx", "gy", "gz"), P(None, "gx", "gy", "gz"), P(), P())
    out_specs = (P(None, "gx", "gy", "gz"), P(None, "gx", "gy", "gz"), P())
    return jax.shard_map(shards, mesh=mesh, in_specs=in_specs, out_specs=out_specs, check_vma=False)
```

profile of v0, /device:TPU:0, one launch (start us, length us, event | category | flops | bytes accessed | tf_op | source)
XLA Modules:
  0.0 144.0 jit_solution(11599108853970660724)
XLA Ops:
  2.5 2.5 %collective-permute-start.1 = (f32[19,2,8,128]{3,1,2,0:T(2,128)S(1)}, f32[19,2,8,128]{3,1,2,0:T(2,128)S(1)}, u32[]{:S(2)}, u32[]{:S(2)}) collective-permute-start(f32[19,2,8,128]{3,1,2,0:T(2,128)S(1)} %get-tuple-element.224), channel_id=1, source_target_pairs={{8,0},{16,8},{24,16},{0,24},{9,1},{17,9},{25,17},{1,25},{10,2},{18... | collective-permute-start | bytes 466952 | tf_op jit(solution)/shard_map/ppermute | solution.py:48
  5.5 1.8 %collective-permute-start.7 = (f32[19,1,4,64]{3,2,1,0:T(4,128)S(1)}, f32[19,1,4,64]{3,2,1,0:T(4,128)S(1)}, u32[]{:S(2)}, u32[]{:S(2)}) collective-permute-start(f32[19,1,4,64]{3,2,1,0:T(4,128)S(1)} %get-tuple-element.247), channel_id=1, source_target_pairs={{8,0},{16,8},{24,16},{0,24},{9,1},{17,9},{25,17},{1,25},{10,2},{18... | collective-permute-start | bytes 58376 | tf_op jit(solution)/shard_map/ppermute | solution.py:48
  11.7 1.6 %collective-permute-start.9 = (f32[19,6,1,64]{3,2,1,0:T(1,128)S(1)}, f32[19,6,1,64]{3,2,1,0:T(1,128)S(1)}, u32[]{:S(2)}, u32[]{:S(2)}) collective-permute-start(f32[19,6,1,64]{3,2,1,0:T(1,128)S(1)} %get-tuple-element.245), channel_id=1, source_target_pairs={{4,0},{0,4},{5,1},{1,5},{6,2},{2,6},{7,3},{3,7},{12,8},{8,12},{13,... | collective-permute-start | bytes 87560 | tf_op jit(solution)/shard_map/ppermute | solution.py:48
  13.9 1.6 %collective-permute-start.3 = (f32[19,8,2,128]{3,1,2,0:T(8,128)S(1)}, f32[19,8,2,128]{3,1,2,0:T(8,128)S(1)}, u32[]{:S(2)}, u32[]{:S(2)}) collective-permute-start(f32[19,8,2,128]{3,1,2,0:T(8,128)S(1)} %get-tuple-element.193), channel_id=1, source_target_pairs={{4,0},{0,4},{5,1},{1,5},{6,2},{2,6},{7,3},{3,7},{12,8},{8,12},{13,... | collective-permute-start | bytes 466952 | tf_op jit(solution)/shard_map/ppermute | solution.py:48
  16.6 1.5 %collective-permute-done.8 = f32[19,6,1,64]{3,2,1,0:T(1,128)S(1)} collective-permute-done((f32[19,6,1,64]{3,2,1,0:T(1,128)S(1)}, f32[19,6,1,64]{3,2,1,0:T(1,128)S(1)}, u32[]{:S(2)}, u32[]{:S(2)}) %collective-permute-start.8) | collective-permute-done | bytes 29216 | tf_op jit(solution)/shard_map/ppermute | solution.py:46
  18.3 3.1 %collective-permute-done.3 = f32[19,8,2,128]{3,1,2,0:T(8,128)S(1)} collective-permute-done((f32[19,8,2,128]{3,1,2,0:T(8,128)S(1)}, f32[19,8,2,128]{3,1,2,0:T(8,128)S(1)}, u32[]{:S(2)}, u32[]{:S(2)}) %collective-permute-start.3) | collective-permute-done | bytes 155680 | tf_op jit(solution)/shard_map/ppermute | solution.py:48
  21.4 2.8 %collective-permute-done.2 = f32[19,8,2,128]{3,1,2,0:T(8,128)S(1)} collective-permute-done((f32[19,8,2,128]{3,1,2,0:T(8,128)S(1)}, f32[19,8,2,128]{3,1,2,0:T(8,128)S(1)}, u32[]{:S(2)}, u32[]{:S(2)}) %collective-permute-start.2) | collective-permute-done | bytes 155680 | tf_op jit(solution)/shard_map/ppermute | solution.py:46
  25.5 1.4 copy.225
  26.9 3.6 %collective-permute-start.5 = (f32[19,8,12,2]{0,1,3,2:T(8,128)}, f32[19,8,12,2]{0,1,3,2:T(8,128)S(1)}, u32[]{:S(2)}, u32[]{:S(2)}) collective-permute-start(f32[19,8,12,2]{0,1,3,2:T(8,128)} %copy.225), channel_id=1, source_target_pairs={{1,0},{2,1},{3,2},{0,3},{5,4},{6,5},{7,6},{4,7},{9,8},{10,9},{11,1... | collective-permute-start | bytes 43784 | tf_op jit(solution)/shard_map/ppermute | solution.py:48
  32.4 3.8 %collective-permute-start.11 = (f32[19,6,6,1]{3,2,1,0:T(8,128)}, f32[19,6,6,1]{3,2,1,0:T(8,128)}, u32[]{:S(2)}, u32[]{:S(2)}) collective-permute-start(f32[19,6,6,1]{3,2,1,0:T(8,128)} %get-tuple-element.218), channel_id=1, source_target_pairs={{1,0},{2,1},{3,2},{0,3},{5,4},{6,5},{7,6},{4,7},{9,8},{10,9},{11,1... | collective-permute-start | bytes 8216 | tf_op jit(solution)/shard_map/ppermute | solution.py:48
  37.2 1.6 %collective-permute-done.4 = f32[19,8,12,2]{0,1,3,2:T(8,128)S(1)} collective-permute-done((f32[19,8,12,2]{0,1,3,2:T(8,128)S(1)}, f32[19,8,12,2]{0,1,3,2:T(8,128)S(1)}, u32[]{:S(2)}, u32[]{:S(2)}) %collective-permute-start.4) | collective-permute-done | bytes 14624 | tf_op jit(solution)/shard_map/ppermute | solution.py:46
  39.8 5.8 %pad_maximum_fusion.11 = (f32[19,1,12,132]{3,1,2,0:T(1,128)}, f32[19,1,12,132]{3,1,2,0:T(1,128)}) fusion(f32[19,8,12,2]{3,1,2,0:T(8,128)S(1)} %copy.227, f32[19,8,12,2]{3,1,2,0:T(8,128)S(1)} %copy.226, f32[19,8,2,128]{3,1,2,0:T(8,128)S(1)} %copy-done.7, f32[19,8,2,128]{3,1,2,0:T(8,128)S(1)} %copy-done.9, f32[19,2,8,128]{3,1,2,0:T(2,128)S(1)} %collective-permute-done.1, ...), kind=kLoop, calls=%fused_computation.30 | loop fusion | flops 361152 | bytes 1203840 | tf_op jit(solution)/shard_map/slice | solution.py:286
  45.6 1.3 copy.231
  46.9 1.4 reshape_squeeze.7
  48.3 2.7 %fusion.15 = f32[19,6,1,66,1]{0,4,3,2,1:T(1,128)} fusion(f32[19,6,2,66,2]{0,4,3,2,1:T(2,128)} %reshape_squeeze.7), kind=kLoop, calls=%fused_computation.32 | loop fusion | flops 30096 | bytes 150480 | tf_op jit(solution)/shard_map/mul | solution.py:160
  52.2 1.4 reshape_squeeze.6
  53.6 2.0 %fusion.16 = f32[19,6,1,66,1]{0,4,3,2,1:T(1,128)S(1)} fusion(f32[19,6,2,66,2]{0,4,3,2,1:T(2,128)} %reshape_squeeze.6), kind=kLoop, calls=%fused_computation.36 | loop fusion | flops 30096 | bytes 150480 | tf_op jit(solution)/shard_map/mul | solution.py:160
  57.5 2.6 %select_select_fusion = (f32[19,6,6,66]{3,2,1,0:T(8,128)}, f32[19,6,6,66]{3,2,1,0:T(8,128)S(1)}) fusion(f32[19,6,66]{2,1,0:T(8,128)S(1)} %bitcast.1004, f32[19,6,66]{2,1,0:T(8,128)} %bitcast.1005, pred[6]{0:T(512)(128)(4,1)S(1)} %copy-done.20, pred[6]{0:T(512)(128)(4,1)S(1)} %copy-done.21, f32[19,6,6,1]{3,2,1,0:T(8,128)} %collective-permute-done.11, ...), kind=kLoop, calls=%fused_computation.16 | loop fusion | flops 361152 | bytes 601932 | tf_op jit(solution)/shard_map/jit(_where)/select_n | solution.py:291
  61.2 1.5 %reshape.517 = f32[19,12,132]{0,2,1:T(8,128)} reshape(f32[19,12,66,2]{0,3,2,1:T(2,128)S(1)} %broadcast_in_dim.149) | data formatting | bytes 240768 | tf_op jit(solution)/shard_map/reshape | solution.py:155
  63.9 1.4 copy.237
  65.8 1.5 %reshape.515 = f32[19,12,132]{0,2,1:T(8,128)} reshape(f32[19,12,66,2]{0,3,2,1:T(2,128)S(1)} %broadcast_in_dim.145) | data formatting | bytes 240768 | tf_op jit(solution)/shard_map/reshape | solution.py:155
  67.2 2.1 %slice.2115 = f32[19,10,130]{0,2,1:T(8,128)} slice(f32[19,12,132]{0,2,1:T(8,128)} %reshape.515), slice={[0:19], [1:11], [1:131]} | slice | bytes 197600 | tf_op jit(solution)/shard_map/slice | solution.py:255
  69.3 1.8 %copy.235 = f32[19,10,130]{2,1,0:T(8,128)S(1)} copy(f32[19,10,130]{0,2,1:T(8,128)} %slice.2115) | data formatting | bytes 197600 | tf_op jit(solution)/shard_map/slice | solution.py:255
  71.1 2.4 %fusion.1 = f32[19,6,10,130]{3,1,2,0:T(8,128)S(1)} fusion(f32[19,8,12,2]{3,1,2,0:T(8,128)S(1)} %copy.227, f32[19,8,12,2]{3,1,2,0:T(8,128)S(1)} %copy.226, f32[19,8,2,128]{3,1,2,0:T(8,128)} %copy-done.6, f32[19,8,2,128]{3,1,2,0:T(8,128)} %copy-done.8, f32[19,2,8,128]{3,1,2,0:T(2,128)S(1)} %collective-permute-done.1, ...), kind=kLoop, calls=%fused_computation.2 | loop fusion | flops 1185600 | bytes 1753484 | tf_op jit(solution)/shard_map/jit(_where)/select_n | solution.py:263
  76.2 1.5 %constant_dynamic-update-slice_fusion.75 = (f32[19,4,8,128]{3,1,2,0:T(4,128)S(1)}, f32[4,8,128]{2,0,1:T(4,128)S(1)}, f32[4,8,128]{2,0,1:T(4,128)S(1)}, f32[4,8,1...) fusion(f32[4,8,128]{2,0,1:T(4,128)S(1)} %get-tuple-element.92, ...), kind=kLoop, calls=%fused_computation.114 | loop fusion | flops 1130495 | bytes 1474560
  80.8 2.6 %collective-permute-done.12 = f32[19,1,8,128]{3,1,2,0:T(1,128)S(1)} collective-permute-done((f32[19,1,8,128]{3,1,2,0:T(1,128)S(1)}, f32[19,1,8,128]{3,1,2,0:T(1,128)S(1)}, u32[]{:S(2)}, u32[]{:S(2)}) %collective-permute-start.12) | collective-permute-done | bytes 77856 | tf_op jit(solution)/shard_map/ppermute | solution.py:46
  83.4 1.4 collective-permute-start.15
  85.9 2.8 %collective-permute-done.15 = f32[19,6,1,128]{3,1,2,0:T(8,128)S(1)} collective-permute-done((f32[19,6,1,128]{3,1,2,0:T(8,128)S(1)}, f32[19,6,1,128]{3,1,2,0:T(8,128)S(1)}, u32[]{:S(2)}, u32[]{:S(2)}) %collective-permute-start.15) | collective-permute-done | bytes 58400 | tf_op jit(solution)/shard_map/ppermute | solution.py:48
  90.5 1.7 %collective-permute-start.17 = (f32[19,6,10,1]{0,3,2,1:T(1,128)S(1)}, f32[19,6,10,1]{0,3,2,1:T(1,128)S(1)}, u32[]{:S(2)}, u32[]{:S(2)}) collective-permute-start(f32[19,6,10,1]{0,3,2,1:T(1,128)S(1)} %copy.242), channel_id=1, source_target_pairs={{1,0},{2,1},{3,2},{0,3},{5,4},{6,5},{7,6},{4,7},{9,8},{10,9},{11,1... | collective-permute-start | bytes 13688 | tf_op jit(solution)/shard_map/ppermute | solution.py:48
  95.1 3.3 %collective-permute-done.16 = f32[19,6,10,1]{0,3,2,1:T(1,128)S(1)} collective-permute-done((f32[19,6,10,1]{0,3,2,1:T(1,128)S(1)}, f32[19,6,10,1]{0,3,2,1:T(1,128)S(1)}, u32[]{:S(2)}, u32[]{:S(2)}) %collective-permute-start.16) | collective-permute-done | bytes 4592 | tf_op jit(solution)/shard_map/ppermute | solution.py:46
  99.0 1.4 fusion.2
  106.6 36.8 %all-reduce.36 = (f32[1,3,1,1,8]{4,1,3,2,0:T(4,128)S(1)}, f32[1,3,1,1,8]{4,1,3,2,0:T(4,128)S(1)}) all-reduce(f32[1,3,1,1,8]{4,1,3,2,0:T(4,128)S(1)} %convolution_bitcast_fusion, f32[1,3,1,1,8]{4,1,3,2,0:T(4,128)S(1)} %convolution_bitcast_fusion.1), channel_id=1, replica_groups=mesh['gx'=4,'gy'=2,'gz'=4] {'gx','gy','gz'}, use_global_device_ids=true, to_apply=%region_1.2 | all-reduce | flops 48 | bytes 384 | tf_op jit(solution)/shard_map/psum | solution.py:229
  (268 shorter events, 38.2 us)
Async XLA Ops:
  1.9 6.6 %copy-start.29 = (f32[3,1,1,8]{3,2,1,0:T(1,128)S(1)}, f32[3,1,1,8]{3,2,1,0:T(1,128)}, u32[]{:S(2)}) copy-start(f32[3,1,1,8]{3,2,1,0:T(1,128)} %param.7) | copy-start | bytes 292
  2.5 11.3 %collective-permute-start.1 = (f32[19,2,8,128]{3,1,2,0:T(2,128)S(1)}, f32[19,2,8,128]{3,1,2,0:T(2,128)S(1)}, u32[]{:S(2)}, u32[]{:S(2)}) collective-permute-start(f32[19,2,8,128]{3,1,2,0:T(2,128)S(1)} %get-tuple-element.224), channel_id=1, source_target_pairs={{8,0},{16,8},{24,16},{0,24},{9,1},{17,9},{25,17},{1,25},{10,2},{18... | collective-permute-start | bytes 466952 | tf_op jit(solution)/shard_map/ppermute | solution.py:48
  4.9 8.9 %collective-permute-start = (f32[19,2,8,128]{3,1,2,0:T(2,128)S(1)}, f32[19,2,8,128]{3,1,2,0:T(2,128)S(1)}, u32[]{:S(2)}, u32[]{:S(2)}) collective-permute-start(f32[19,2,8,128]{3,1,2,0:T(2,128)S(1)} %get-tuple-element.223), channel_id=1, source_target_pairs={{0,8},{8,16},{16,24},{24,0},{1,9},{9,17},{17,25},{25,1},{2,10},{10... | collective-permute-start | bytes 466952 | tf_op jit(solution)/shard_map/ppermute | solution.py:46
  5.4 19.8 %copy-start.3 = (f32[19,4,4,64]{3,2,1,0:T(4,128)}, f32[19,4,4,64]{3,2,1,0:T(4,128)S(1)}, u32[]{:S(2)}) copy-start(f32[19,4,4,64]{3,2,1,0:T(4,128)S(1)} %constant_dynamic-update-slice_fusion.19) | copy-start | bytes 233476
  5.5 6.1 %collective-permute-start.7 = (f32[19,1,4,64]{3,2,1,0:T(4,128)S(1)}, f32[19,1,4,64]{3,2,1,0:T(4,128)S(1)}, u32[]{:S(2)}, u32[]{:S(2)}) collective-permute-start(f32[19,1,4,64]{3,2,1,0:T(4,128)S(1)} %get-tuple-element.247), channel_id=1, source_target_pairs={{8,0},{16,8},{24,16},{0,24},{9,1},{17,9},{25,17},{1,25},{10,2},{18... | collective-permute-start | bytes 58376 | tf_op jit(solution)/shard_map/ppermute | solution.py:48
  7.2 4.3 %collective-permute-start.6 = (f32[19,1,4,64]{3,2,1,0:T(4,128)S(1)}, f32[19,1,4,64]{3,2,1,0:T(4,128)S(1)}, u32[]{:S(2)}, u32[]{:S(2)}) collective-permute-start(f32[19,1,4,64]{3,2,1,0:T(4,128)S(1)} %get-tuple-element.246), channel_id=1, source_target_pairs={{0,8},{8,16},{16,24},{24,0},{1,9},{9,17},{17,25},{25,1},{2,10},{10... | collective-permute-start | bytes 58376 | tf_op jit(solution)/shard_map/ppermute | solution.py:46
  10.8 5.8 %copy-start.18 = (pred[8,12,132]{2,0,1:T(8,128)(4,1)}, pred[8,12,132]{2,0,1:T(8,128)(4,1)S(1)}, u32[]{:S(2)}) copy-start(pred[8,12,132]{2,0,1:T(8,128)(4,1)S(1)} %get-tuple-element.252) | copy-start | bytes 38020
  11.6 13.6 %copy-start.11 = (f32[19,1,4,64]{3,2,1,0:T(4,128)}, f32[19,1,4,64]{3,2,1,0:T(4,128)S(1)}, u32[]{:S(2)}) copy-start(f32[19,1,4,64]{3,2,1,0:T(4,128)S(1)} %collective-permute-done.7) | copy-start | bytes 58372
  11.6 12.7 %copy-start.13 = (f32[19,1,4,64]{3,2,1,0:T(4,128)}, f32[19,1,4,64]{3,2,1,0:T(4,128)S(1)}, u32[]{:S(2)}) copy-start(f32[19,1,4,64]{3,2,1,0:T(4,128)S(1)} %collective-permute-done.6) | copy-start | bytes 58372
  11.7 4.9 %collective-permute-start.9 = (f32[19,6,1,64]{3,2,1,0:T(1,128)S(1)}, f32[19,6,1,64]{3,2,1,0:T(1,128)S(1)}, u32[]{:S(2)}, u32[]{:S(2)}) collective-permute-start(f32[19,6,1,64]{3,2,1,0:T(1,128)S(1)} %get-tuple-element.245), channel_id=1, source_target_pairs={{4,0},{0,4},{5,1},{1,5},{6,2},{2,6},{7,3},{3,7},{12,8},{8,12},{13,... | collective-permute-start | bytes 87560 | tf_op jit(solution)/shard_map/ppermute | solution.py:48
  13.3 4.8 %collective-permute-start.8 = (f32[19,6,1,64]{3,2,1,0:T(1,128)S(1)}, f32[19,6,1,64]{3,2,1,0:T(1,128)S(1)}, u32[]{:S(2)}, u32[]{:S(2)}) collective-permute-start(f32[19,6,1,64]{3,2,1,0:T(1,128)S(1)} %get-tuple-element.244), channel_id=1, source_target_pairs={{0,4},{4,0},{1,5},{5,1},{2,6},{6,2},{3,7},{7,3},{8,12},{12,8},{9,1... | collective-permute-start | bytes 87560 | tf_op jit(solution)/shard_map/ppermute | solution.py:46
  13.8 26.0 %copy-start.1 = (f32[19,2,8,128]{3,1,2,0:T(2,128)}, f32[19,2,8,128]{3,1,2,0:T(2,128)S(1)}, u32[]{:S(2)}) copy-start(f32[19,2,8,128]{3,1,2,0:T(2,128)S(1)} %collective-permute-done) | copy-start | bytes 466948
  13.9 7.5 %collective-permute-start.3 = (f32[19,8,2,128]{3,1,2,0:T(8,128)S(1)}, f32[19,8,2,128]{3,1,2,0:T(8,128)S(1)}, u32[]{:S(2)}, u32[]{:S(2)}) collective-permute-start(f32[19,8,2,128]{3,1,2,0:T(8,128)S(1)} %get-tuple-element.193), channel_id=1, source_target_pairs={{4,0},{0,4},{5,1},{1,5},{6,2},{2,6},{7,3},{3,7},{12,8},{8,12},{13,... | collective-permute-start | bytes 466952 | tf_op jit(solution)/shard_map/ppermute | solution.py:48
  15.5 8.8 %collective-permute-start.2 = (f32[19,8,2,128]{3,1,2,0:T(8,128)S(1)}, f32[19,8,2,128]{3,1,2,0:T(8,128)S(1)}, u32[]{:S(2)}, u32[]{:S(2)}) collective-permute-start(f32[19,8,2,128]{3,1,2,0:T(8,128)S(1)} %get-tuple-element.192), channel_id=1, source_target_pairs={{0,4},{4,0},{1,5},{5,1},{2,6},{6,2},{3,7},{7,3},{8,12},{12,8},{9,1... | collective-permute-start | bytes 466952 | tf_op jit(solution)/shard_map/ppermute | solution.py:46
  16.6 7.7 %copy-start.16 = (f32[19,6,1,64]{3,2,1,0:T(1,128)}, f32[19,6,1,64]{3,2,1,0:T(1,128)S(1)}, u32[]{:S(2)}) copy-start(f32[19,6,1,64]{3,2,1,0:T(1,128)S(1)} %collective-permute-done.9) | copy-start | bytes 87556
  18.1 6.2 %copy-start.17 = (f32[19,6,1,64]{3,2,1,0:T(1,128)}, f32[19,6,1,64]{3,2,1,0:T(1,128)S(1)}, u32[]{:S(2)}) copy-start(f32[19,6,1,64]{3,2,1,0:T(1,128)S(1)} %collective-permute-done.8) | copy-start | bytes 87556
  26.9 9.3 %collective-permute-start.5 = (f32[19,8,12,2]{0,1,3,2:T(8,128)}, f32[19,8,12,2]{0,1,3,2:T(8,128)S(1)}, u32[]{:S(2)}, u32[]{:S(2)}) collective-permute-start(f32[19,8,12,2]{0,1,3,2:T(8,128)} %copy.225), channel_id=1, source_target_pairs={{1,0},{2,1},{3,2},{0,3},{5,4},{6,5},{7,6},{4,7},{9,8},{10,9},{11,1... | collective-permute-start | bytes 43784 | tf_op jit(solution)/shard_map/ppermute | solution.py:48
  31.3 8.5 %copy-start.7 = (f32[19,8,2,128]{3,1,2,0:T(8,128)S(1)}, f32[19,8,2,128]{3,1,2,0:T(8,128)}, u32[]{:S(2)}) copy-start(f32[19,8,2,128]{3,1,2,0:T(8,128)} %copy-done.6) | copy-start | bytes 466948
  31.3 8.5 %copy-start.9 = (f32[19,8,2,128]{3,1,2,0:T(8,128)S(1)}, f32[19,8,2,128]{3,1,2,0:T(8,128)}, u32[]{:S(2)}) copy-start(f32[19,8,2,128]{3,1,2,0:T(8,128)} %copy-done.8) | copy-start | bytes 466948
  31.3 7.5 %collective-permute-start.4 = (f32[19,8,12,2]{0,1,3,2:T(8,128)S(1)}, f32[19,8,12,2]{0,1,3,2:T(8,128)S(1)}, u32[]{:S(2)}, u32[]{:S(2)}) collective-permute-start(f32[19,8,12,2]{0,1,3,2:T(8,128)S(1)} %copy.224), channel_id=1, source_target_pairs={{0,1},{1,2},{2,3},{3,0},{4,5},{5,6},{6,7},{7,4},{8,9},{9,10},{10,1... | collective-permute-start | bytes 43784 | tf_op jit(solution)/shard_map/ppermute | solution.py:46
  32.4 25.1 %collective-permute-start.11 = (f32[19,6,6,1]{3,2,1,0:T(8,128)}, f32[19,6,6,1]{3,2,1,0:T(8,128)}, u32[]{:S(2)}, u32[]{:S(2)}) collective-permute-start(f32[19,6,6,1]{3,2,1,0:T(8,128)} %get-tuple-element.218), channel_id=1, source_target_pairs={{1,0},{2,1},{3,2},{0,3},{5,4},{6,5},{7,6},{4,7},{9,8},{10,9},{11,1... | collective-permute-start | bytes 8216 | tf_op jit(solution)/shard_map/ppermute | solution.py:48
  36.2 21.3 %collective-permute-start.10 = (f32[19,6,6,1]{3,2,1,0:T(8,128)}, f32[19,6,6,1]{3,2,1,0:T(8,128)}, u32[]{:S(2)}, u32[]{:S(2)}) collective-permute-start(f32[19,6,6,1]{3,2,1,0:T(8,128)} %get-tuple-element.217), channel_id=1, source_target_pairs={{0,1},{1,2},{2,3},{3,0},{4,5},{5,6},{6,7},{7,4},{8,9},{9,10},{10,1... | collective-permute-start | bytes 8216 | tf_op jit(solution)/shard_map/ppermute | solution.py:46
  77.9 7.6 %copy-start.19 = (f32[10,6,1,1]{1,0,2,3:T(8,128)S(1)}, f32[10,6,1,1]{1,0,2,3:T(8,128)}, u32[]{:S(2)}) copy-start(f32[10,6,1,1]{1,0,2,3:T(8,128)} %multiply_bitcast_fusion.3) | copy-start | bytes 724
  78.4 2.4 %collective-permute-start.13 = (f32[19,1,8,128]{3,1,2,0:T(1,128)S(1)}, f32[19,1,8,128]{3,1,2,0:T(1,128)S(1)}, u32[]{:S(2)}, u32[]{:S(2)}) collective-permute-start(f32[19,1,8,128]{3,1,2,0:T(1,128)S(1)} %get-tuple-element.222), channel_id=1, source_target_pairs={{8,0},{16,8},{24,16},{0,24},{9,1},{17,9},{25,17},{1,25},{10,2},{18... | collective-permute-start | bytes 233480 | tf_op jit(solution)/shard_map/ppermute | solution.py:48
  78.8 4.6 %collective-permute-start.12 = (f32[19,1,8,128]{3,1,2,0:T(1,128)S(1)}, f32[19,1,8,128]{3,1,2,0:T(1,128)S(1)}, u32[]{:S(2)}, u32[]{:S(2)}) collective-permute-start(f32[19,1,8,128]{3,1,2,0:T(1,128)S(1)} %get-tuple-element.221), channel_id=1, source_target_pairs={{0,8},{8,16},{16,24},{24,0},{1,9},{9,17},{17,25},{25,1},{2,10},{10... | collective-permute-start | bytes 233480 | tf_op jit(solution)/shard_map/ppermute | solution.py:46
  80.1 9.6 %copy-start.27 = (f32[19,4,4,64]{3,2,1,0:T(4,128)}, f32[19,4,4,64]{3,2,1,0:T(4,128)S(1)}, u32[]{:S(2)}) copy-start(f32[19,4,4,64]{3,2,1,0:T(4,128)S(1)} %constant_dynamic-update-slice_fusion.38) | copy-start | bytes 233476
  83.4 5.2 %collective-permute-start.15 = (f32[19,6,1,128]{3,1,2,0:T(8,128)S(1)}, f32[19,6,1,128]{3,1,2,0:T(8,128)S(1)}, u32[]{:S(2)}, u32[]{:S(2)}) collective-permute-start(f32[19,6,1,128]{3,1,2,0:T(8,128)S(1)} %get-tuple-element.195), channel_id=1, source_target_pairs={{4,0},{0,4},{5,1},{1,5},{6,2},{2,6},{7,3},{3,7},{12,8},{8,12},{13,... | collective-permute-start | bytes 175112 | tf_op jit(solution)/shard_map/ppermute | solution.py:48
  84.8 4.6 %collective-permute-start.14 = (f32[19,6,1,128]{3,1,2,0:T(8,128)S(1)}, f32[19,6,1,128]{3,1,2,0:T(8,128)S(1)}, u32[]{:S(2)}, u32[]{:S(2)}) collective-permute-start(f32[19,6,1,128]{3,1,2,0:T(8,128)S(1)} %get-tuple-element.194), channel_id=1, source_target_pairs={{0,4},{4,0},{1,5},{5,1},{2,6},{6,2},{3,7},{7,3},{8,12},{12,8},{9,1... | collective-permute-start | bytes 175112 | tf_op jit(solution)/shard_map/ppermute | solution.py:46
  90.0 9.1 %copy-start.24 = (pred[6]{0:T(512)(128)(4,1)S(1)}, pred[6]{0:T(512)(128)(4,1)}, u32[]{:S(2)}) copy-start(pred[6]{0:T(512)(128)(4,1)} %get-tuple-element.256) | copy-start | bytes 22
  90.0 9.1 %copy-start.26 = (pred[6]{0:T(512)(128)(4,1)S(1)}, pred[6]{0:T(512)(128)(4,1)}, u32[]{:S(2)}) copy-start(pred[6]{0:T(512)(128)(4,1)} %get-tuple-element.257) | copy-start | bytes 22
  90.5 3.9 %collective-permute-start.17 = (f32[19,6,10,1]{0,3,2,1:T(1,128)S(1)}, f32[19,6,10,1]{0,3,2,1:T(1,128)S(1)}, u32[]{:S(2)}, u32[]{:S(2)}) collective-permute-start(f32[19,6,10,1]{0,3,2,1:T(1,128)S(1)} %copy.242), channel_id=1, source_target_pairs={{1,0},{2,1},{3,2},{0,3},{5,4},{6,5},{7,6},{4,7},{9,8},{10,9},{11,1... | collective-permute-start | bytes 13688 | tf_op jit(solution)/shard_map/ppermute | solution.py:48
  92.7 5.7 %collective-permute-start.16 = (f32[19,6,10,1]{0,3,2,1:T(1,128)S(1)}, f32[19,6,10,1]{0,3,2,1:T(1,128)S(1)}, u32[]{:S(2)}, u32[]{:S(2)}) collective-permute-start(f32[19,6,10,1]{0,3,2,1:T(1,128)S(1)} %copy.241), channel_id=1, source_target_pairs={{0,1},{1,2},{2,3},{3,0},{4,5},{5,6},{6,7},{7,4},{8,9},{9,10},{10,1... | collective-permute-start | bytes 13688 | tf_op jit(solution)/shard_map/ppermute | solution.py:46
  (16 other events, 55.9 us)
where the time goes:
time: 145 us; the launch traced here: 144 us
  blocking collectives  36.8 us (25%)
  other arithmetic  31.7 us (22%)
  local copies, waits for them, and re-layouts  30.9 us (21%)
  starting transfers between devices  20.7 us (14%)
  waiting for transfers between devices  19.9 us (14%)
  matrix products  2.62 us (2%)
  between operations  1.46 us (1%)
    psum x1, blocking collectives, reduce_forces(): return lax.psum(forces, ('gx', 'gy', 'gz'))  36.8 us
    ppermute x9, starting transfers between devices, extended(): lax.ppermute(head, axis, [((i + 1) % count, i) for i in range(count)])  18.3 us
    ppermute x9, waiting for transfers between devices, extended(): lax.ppermute(tail, axis, [(i, (i + 1) % count) for i in range(count)])  12.7 us
    ppermute x9, waiting for transfers between devices, extended(): lax.ppermute(head, axis, [((i + 1) % count, i) for i in range(count)])  7.18 us
    unnamed x72, other arithmetic  5.9 us
    slice x1, other arithmetic, shards(): left_coal = coalesce(first_post[:, 1])  5.81 us
    mul x2, other arithmetic, coalesce(): (grouped[:, :, 0, :, 0] + grouped[:, :, 1, :, 0] + grouped[:, :, 0, :, 1]...  4.64 us
    slice x2, local copies, waits for them, and re-layouts, with_explosion(): left_fill[:, trim_by:left_fill.shape[1] - trim_by, trim_by:left_fill.shap...  3.83 us
  transfers between devices with their start and end apart: 18, of which 10 were waited for; matrix products, arithmetic and copies ran while one was open for 21% of the time, Pallas kernels for 0%

commit v1 on v0

v1 whole, which is shorter than its diff:
```python
import functools

import jax
import jax.numpy as jnp
from jax import lax
from jax.experimental import pallas as pl
from jax.experimental.pallas import tpu as pltpu
from jax.sharding import PartitionSpec as P

BOX_XY = 16
BOX_Z = 64
RADIUS = 4
VELOCITIES = (
    (0, 0, 0),
    (1, 0, 0),
    (-1, 0, 0),
    (0, 1, 0),
    (0, -1, 0),
    (0, 0, 1),
    (0, 0, -1),
    (1, 1, 0),
    (-1, -1, 0),
    (1, -1, 0),
    (-1, 1, 0),
    (1, 0, 1),
    (-1, 0, -1),
    (1, 0, -1),
    (-1, 0, 1),
    (0, 1, 1),
    (0, -1, -1),
    (0, 1, -1),
    (0, -1, 1),
)
OPPOSITE = (0, 2, 1, 4, 3, 6, 5, 8, 7, 10, 9, 12, 11, 14, 13, 16, 15, 18, 17)
WEIGHTS = (1.0 / 3.0,) + (1.0 / 18.0,) * 6 + (1.0 / 36.0,) * 12
COARSE_RATE = 1.25
FINE_RATE = 1.0 / 1.1
HIGHEST = lax.Precision.HIGHEST
MESH = pl.DeviceIdType.MESH
AXES = ("gx", "gy", "gz")
DIRS = VELOCITIES[1:]
RHO = 5
MOVERS = {
    (axis, sign): tuple(q for q in range(19) if VELOCITIES[q][axis] == sign)
    for axis in range(3)
    for sign in (1, -1)
}
SLOT = {1: 0, -1: 1}
PAIRS = ((1, 1), (1, -1), (-1, 1), (-1, -1))
PAIR_SLOT = {pair: i for i, pair in enumerate(PAIRS)}
FIRST_ROW = 8
COARSE_ROW = 32
ROWS = 52
LANES = 128
SUB = 8


def iota(shape, axis):
    return lax.broadcasted_iota(jnp.int32, shape, axis)


def project(vectors, direction):
    total = None
    for dim in range(3):
        sign = VELOCITIES[direction][dim]
        if sign == 1:
            total = vectors[dim] if total is None else total + vectors[dim]
        elif sign == -1:
            total = -vectors[dim] if total is None else total - vectors[dim]
    return total


def collide(read, write, rate):
    density = read(0)
    momentum = [None, None, None]
    for q in range(1, 19):
        value = read(q)
        density = density + value
        for dim in range(3):
            sign = VELOCITIES[q][dim]
            if sign:
                if momentum[dim] is None:
                    momentum[dim] = value if sign == 1 else -value
                else:
                    momentum[dim] = momentum[dim] + value if sign == 1 else momentum[dim] - value
    inverse = 1.0 / density
    velocity = [m * inverse for m in momentum]
    base = 1.0 - 1.5 * (
        velocity[0] * velocity[0] + velocity[1] * velocity[1] + velocity[2] * velocity[2]
    )
    scaled = {w: (rate * w) * density for w in set(WEIGHTS)}
    keep = 1.0 - rate
    write(0, keep * read(0) + scaled[WEIGHTS[0]] * base)
    for q in range(1, 19, 2):
        along = project(velocity, q)
        even = base + 4.5 * along * along
        odd = 3.0 * along
        weight = scaled[WEIGHTS[q]]
        write(q, keep * read(q) + weight * (even + odd))
        write(q + 1, keep * read(q + 1) + weight * (even - odd))
    return density


class Halo:
    def __init__(self, send, recv):
        self.sx, self.sy, self.sz = send
        self.rx, self.ry, self.rz, self.rxy, self.rxz, self.ryz = recv

    def pack(self, own, edge_planes, with_rho, rows, lanes, part):
        x0 = 0 if part == 0 else 6
        y0 = FIRST_ROW if part == 0 else COARSE_ROW
        lane = iota((SUB, LANES), 1)
        for sign in (1, -1):
            for k, q in enumerate(MOVERS[0, sign] + ((RHO + 100,) if with_rho else ())):
                self.sx[SLOT[sign], x0 + k] = edge_planes[sign](q)
        for sign in (1, -1):
            row = rows - 1 if sign == 1 else 0
            out = SLOT[sign]
            for k, q in enumerate(MOVERS[1, sign] + ((RHO + 100,) if with_rho else ())):
                self.sy[out, y0 + 4 * k : y0 + 4 * k + 4] = own(q)[:, row : row + 1, :]
            for e, xs in enumerate((1, -1)):
                q = VELOCITIES.index((xs, sign, 0))
                if part == 0:
                    self.sy[out, 2 * e] = edge_planes[xs](q)[row : row + 1, :]
                    self.sy[out, 2 * e + 1] = edge_planes[xs](RHO + 100)[row : row + 1, :]
                else:
                    self.sy[out, 4 + e] = edge_planes[xs](q)[row : row + 1, :]
        for sign in (1, -1):
            source = lanes - 1 if sign == 1 else 0
            packed = jnp.zeros((SUB, LANES), jnp.float32)
            for k, q in enumerate(MOVERS[2, sign] + ((RHO + 100,) if with_rho else ())):
                value = own(q)
                for j in range(4):
                    place = k * 6 + j + 1
                    moved = pltpu.roll(value[j], (place - source) % LANES, 1)
                    packed = jnp.where(lane == place, moved, packed)
                for xs, place in ((1, k * 6 + 5), (-1, k * 6)):
                    if q == RHO + 100 or VELOCITIES[q][0] == xs:
                        moved = pltpu.roll(edge_planes[xs](q), (place - source) % LANES, 1)
                        packed = jnp.where(lane == place, moved, packed)
            self.sz[SLOT[sign], part] = packed

    def pull(self, own, c, q, rows, lanes, part):
        cx, cy, cz = c
        is_rho = q == RHO + 100
        x0 = 0 if part == 0 else 6
        y0 = FIRST_ROW if part == 0 else COARSE_ROW

        def index(axis, sign):
            return RHO if is_rho else MOVERS[axis, sign].index(q)

        def along_x(inner, halo):
            if cx == 1:
                return jnp.concatenate([halo, inner[:3]], axis=0)
            return jnp.concatenate([inner[1:], halo], axis=0)

        value = own
        row = iota((1, SUB, 1), 1)
        if cx:
            value = along_x(own, self.rx[SLOT[cx], x0 + index(0, cx)][None])
        if cy:
            edge = 0 if cy == 1 else rows - 1
            k = y0 + 4 * index(1, cy)
            lines = self.ry[SLOT[cy], k : k + 4]
            if cx:
                e = 0 if cx == 1 else 1
                at = (2 * e + (1 if is_rho else 0)) if part == 0 else 4 + e
                lines = along_x(lines, self.rxy[PAIR_SLOT[cx, cy], at : at + 1])
            value = jnp.where(row == edge, lines, pltpu.roll(value, cy % SUB, 1))
        if cz:
            edge = 0 if cz == 1 else lanes - 1
            k = index(2, cz) * 6
            packed = self.rz[SLOT[cz], part]
            if cy:
                source_row = rows - 1 if cy == 1 else 0
                other = self.ryz[PAIR_SLOT[cy, cz], part][source_row : source_row + 1, :]
                edge_row = 0 if cy == 1 else rows - 1
                packed = jnp.where(
                    iota((SUB, 1), 0) == edge_row, other, pltpu.roll(packed, cy % SUB, 0)
                )
            columns = []
            for ix in range(4):
                j = ix - cx
                if 0 <= j < 4:
                    columns.append(pltpu.roll(packed, (edge - (k + j + 1)) % LANES, 1))
                else:
                    other = self.rxz[PAIR_SLOT[cx, cz], part]
                    place = k + 5 if cx == 1 else k
                    columns.append(pltpu.roll(other, (edge - place) % LANES, 1))
            columns = jnp.stack(columns)
            lane = iota((1, 1, LANES), 2)
            value = jnp.where(lane == edge, columns, pltpu.roll(value, cz % LANES, 2))
        return value


def neighbour(c, counts, me):
    return tuple(lax.rem(me[a] + c[a] + counts[a], counts[a]) for a in range(3))


def kernel(
    counts,
    coarse_in,
    fine_in,
    centers,
    speeds,
    coarse_out,
    fine_out,
    force_out,
    fine_a,
    fine_b,
    coarse,
    sx1,
    sy1,
    sz1,
    rx1,
    ry1,
    rz1,
    rxy1,
    rxz1,
    ryz1,
    sx2,
    sy2,
    sz2,
    rx2,
    ry2,
    rz2,
    rxy2,
    rxz2,
    ryz2,
    opens,
    news,
    own_masks,
    dens,
    fill_ref,
    force_own,
    force_x,
    force_y,
    force_z,
    send_sem,
    recv_sem,
    fsend_sem,
    frecv_x,
    frecv_y,
    frecv_z,
):
    me = tuple(lax.axis_index(a) for a in AXES)
    own_x, own_y, own_z = fine_in.shape[1], fine_in.shape[2], fine_in.shape[3]
    rows_c, lanes_c = coarse_in.shape[2], coarse_in.shape[3]
    total_x = own_x * counts[0]
    box_x, box_y, box_z = centers.shape[2], centers.shape[3], centers.shape[4]
    local_z = own_z // BOX_Z

    barrier = pltpu.get_barrier_semaphore()
    for c in DIRS:
        pl.semaphore_signal(
            barrier, inc=1, device_id=neighbour(c, counts, me), device_id_type=MESH
        )
    for axis in range(3):
        for step in range(1, counts[axis]):
            c = tuple(step if a == axis else 0 for a in range(3))
            pl.semaphore_signal(
                barrier, inc=1, device_id=neighbour(c, counts, me), device_id_type=MESH
            )

    def write_a(q, value):
        fine_a[q] = value

    rho = collide(lambda q: fine_in[q], write_a, FINE_RATE)
    coarse[...] = jnp.ones(coarse.shape, jnp.float32)
    coarse[:, :, 0:rows_c, 0:lanes_c] = coarse_in[...]

    def write_c(q, value):
        coarse[q] = value

    rho_c = collide(lambda q: coarse[q], write_c, COARSE_RATE)
    first = me[0] == 0
    last = me[0] == counts[0] - 1
    row3 = iota((1, SUB, 1), 1)

    planes = []
    for sign, ix in ((1, 3), (-1, 0)):
        planes += [coarse[q, ix] for q in MOVERS[0, sign]] + [rho_c[ix]]
    grow = (iota((LANES, LANES), 0) == (iota((LANES, LANES), 1) >> 1)).astype(jnp.float32)
    wide = jnp.dot(
        jnp.concatenate(planes, axis=0), grow, precision=HIGHEST, preferred_element_type=jnp.float32
    ).reshape(12, SUB, LANES)
    tall = wide[:, 3:4, :]
    for r in (2, 1, 0):
        tall = jnp.where(row3 < 2 * r + 2, wide[:, r : r + 1, :], tall)
    fill_ref[...] = tall

    planes = []
    for sign, ix in ((1, 3), (-1, 0)):
        for q in MOVERS[0, sign]:
            plane = fine_a[q, ix]
            planes.append(plane + pltpu.roll(plane, SUB - 1, 0))
    shrink = 0.25 * ((iota((LANES, LANES), 0) >> 1) == iota((LANES, LANES), 1)).astype(jnp.float32)
    thin = jnp.dot(
        jnp.concatenate(planes, axis=0),
        shrink,
        precision=HIGHEST,
        preferred_element_type=jnp.float32,
    ).reshape(10, SUB, LANES)
    flat = thin[:, 6:7, :]
    for r in (2, 1, 0):
        flat = jnp.where(row3 <= r, thin[:, 2 * r : 2 * r + 1, :], flat)

    def fine_edges(ref, density):
        def plane(sign):
            ix, at_end, base = (3, last, 0) if sign == 1 else (0, first, 6)

            def get(q):
                is_rho = q == RHO + 100
                k = RHO if is_rho else MOVERS[0, sign].index(q)
                mine = density[ix] if is_rho else ref[q, ix]
                return jnp.where(at_end, fill_ref[base + k], mine)

            return get

        return {1: plane(1), -1: plane(-1)}

    def coarse_edge(sign):
        ix, at_end, base = (3, last, 0) if sign == 1 else (0, first, 5)

        def get(q):
            return jnp.where(at_end, flat[base + MOVERS[0, sign].index(q)], coarse[q, ix])

        return get

    halo1 = Halo((sx1, sy1, sz1), (rx1, ry1, rz1, rxy1, rxz1, ryz1))
    halo2 = Halo((sx2, sy2, sz2), (rx2, ry2, rz2, rxy2, rxz2, ryz2))
    halo1.pack(
        lambda q: rho if q == RHO + 100 else fine_a[q],
        fine_edges(fine_a, rho),
        True,
        own_y,
        own_z,
        0,
    )
    halo1.pack(
        lambda q: coarse[q],
        {1: coarse_edge(1), -1: coarse_edge(-1)},
        False,
        rows_c,
        lanes_c,
        1,
    )

    def copies(halo, phase):
        made = []
        for i, c in enumerate(DIRS):
            cx, cy, cz = c
            if cz:
                if cx:
                    dst = halo.rxz.at[PAIR_SLOT[cx, cz]]
                elif cy:
                    dst = halo.ryz.at[PAIR_SLOT[cy, cz]]
                else:
                    dst = halo.rz.at[SLOT[cz]]
                src = halo.sz.at[SLOT[cz]]
            elif cy:
                if cx:
                    src = halo.sy.at[SLOT[cy], pl.ds(0, FIRST_ROW)]
                    dst = halo.rxy.at[PAIR_SLOT[cx, cy]]
                else:
                    src = halo.sy.at[SLOT[cy]]
                    dst = halo.ry.at[SLOT[cy]]
            else:
                src = halo.sx.at[SLOT[cx]]
                dst = halo.rx.at[SLOT[cx]]
            made.append(
                pltpu.make_async_remote_copy(
                    src_ref=src,
                    dst_ref=dst,
                    send_sem=send_sem.at[phase, i],
                    recv_sem=recv_sem.at[phase, i],
                    device_id=neighbour(c, counts, me),
                    device_id_type=MESH,
                )
            )
        return made

    pl.semaphore_wait(barrier, 18 + sum(n - 1 for n in counts))
    sends1 = copies(halo1, 0)
    for copy in sends1:
        copy.start()

    start_x, start_y, start_z = me[0] * own_x, me[1] * own_y, me[2] * own_z
    total_y = own_y * counts[1]
    bx0 = lax.div(start_x, BOX_XY)
    by0 = lax.div(start_y, BOX_XY)
    bz0 = me[2] * local_z
    bx_near = {
        1: lax.div(lax.max(start_x - 1, 0), BOX_XY),
        -1: lax.min(lax.div(start_x + own_x, BOX_XY), box_x - 1),
        0: bx0,
    }
    by_near = {
        1: lax.div(lax.rem(start_y + total_y - 1, total_y), BOX_XY),
        -1: lax.div(lax.rem(start_y + own_y, total_y), BOX_XY),
        0: by0,
    }
    bz_all = [lax.rem(bz0 + box_z + i, box_z) for i in range(-1, local_z + 1)]
    lane3 = iota((1, 1, LANES), 2)
    plane3 = iota((own_x, 1, LANES), 0)
    memo = {}

    def along_lanes(get, key, bx_key, by_key, cz):
        full = (key, bx_key, by_key, cz)
        if full in memo:
            return memo[full]
        bx, by = bx_near[bx_key], by_near[by_key]
        at = lane3 - cz
        value = jnp.full((1, 1, LANES), get(bx, by, bz_all[1]))
        for i in range(1, local_z):
            value = jnp.where(at >= i * BOX_Z, get(bx, by, bz_all[1 + i]), value)
        if cz == 1:
            value = jnp.where(at < 0, get(bx, by, bz_all[0]), value)
        elif cz == -1:
            value = jnp.where(at >= own_z, get(bx, by, bz_all[-1]), value)
        value = value.astype(jnp.float32)
        memo[full] = value
        return value

    def box_field(get, key, c):
        cx, cy, cz = c

        def on_rows(bx_key):
            own = along_lanes(get, key, bx_key, 0, cz)
            if cy == 0 or box_y == 1:
                return own
            edge = 0 if cy == 1 else own_y - 1
            return jnp.where(row3 == edge, along_lanes(get, key, bx_key, cy, cz), own)

        if cx == 0 or box_x == 1:
            return on_rows(0)
        edge = 0 if cx == 1 else own_x - 1
        return jnp.where(plane3 == edge, on_rows(cx), on_rows(0))

    def center_getter(moment, dim):
        return lambda bx, by, bz: centers[moment, dim, bx, by, bz]

    def speed_getter(dim):
        return lambda bx, by, bz: speeds[dim, bx, by, bz]

    def speeds_at(c):
        return [box_field(speed_getter(dim), ("u", dim), c) for dim in range(3)]

    def inside_at(cx):
        at = start_x + plane3 - cx
        return (at >= 0) & (at < total_x)

    def solids_at(c):
        cx, cy, cz = c
        off_x = ((start_x + plane3 - cx) & (BOX_XY - 1)).astype(jnp.float32)
        off_y = ((start_y + iota((1, SUB, LANES), 1) - cy) & (BOX_XY - 1)).astype(jnp.float32)
        off_z = ((lane3 - cz) & (BOX_Z - 1)).astype(jnp.float32)
        found = []
        for moment in range(3):
            gap_x = off_x - box_field(center_getter(moment, 0), (moment, 0), c)
            gap_y = off_y - box_field(center_getter(moment, 1), (moment, 1), c)
            gap_z = off_z - box_field(center_getter(moment, 2), (moment, 2), c)
            distance = (gap_x * gap_x + gap_z * gap_z) + gap_y * gap_y
            if cx:
                distance = jnp.where(inside_at(cx), distance, 1e9)
            found.append(jnp.where(distance <= float(RADIUS * RADIUS), 1.0, 0.0))
        return found

    own_solids = solids_at((0, 0, 0))
    for moment in range(3):
        own_masks[moment] = own_solids[moment]
    sums = [jnp.full((own_x, SUB, LANES), WEIGHTS[0], jnp.float32) for s in range(2)]
    for q in range(1, 19):
        s0, s1, s2 = solids_at(VELOCITIES[q])
        for s, (before, after) in enumerate(((s0, s1), (s1, s2))):
            free = (1.0 - before) * (1.0 - after)
            opens[s, q - 1] = free
            news[s, q - 1] = after
            sums[s] = sums[s] + WEIGHTS[q] * free
    for s in range(2):
        dens[s] = sums[s]
    own_speed = speeds_at((0, 0, 0))
    quiet = 1.0 - 1.5 * (
        own_speed[0] * own_speed[0] + own_speed[1] * own_speed[1] + own_speed[2] * own_speed[2]
    )

    def substep(s, halo, ref, density, write):
        covered = own_masks[s + 1] > 0.5
        uncovered = own_masks[s] > 0.5
        push = [jnp.zeros((own_x, SUB, LANES), jnp.float32) for d in range(3)]
        numerator = WEIGHTS[0] * density
        for q in range(1, 19):
            c = VELOCITIES[q]
            near = halo.pull(density, c, RHO + 100, own_y, own_z, 0)
            free = opens[s, q - 1]
            freed = near * free
            numerator = numerator + WEIGHTS[q] * freed
            arrived = halo.pull(ref[q], c, q, own_y, own_z, 0)
            here = (6.0 * WEIGHTS[q]) * project(own_speed, q)
            link = (2.0 * arrived - here * near) * free
            if c[0]:
                link = jnp.where(inside_at(c[0]), link, 0.0)
            for d in range(3):
                if c[d] == 1:
                    push[d] = push[d] + link
                elif c[d] == -1:
                    push[d] = push[d] - link
            wall = (6.0 * WEIGHTS[q]) * project(speeds_at(c), q)
            bounced = ref[OPPOSITE[q]] + density * wall
            arrived = jnp.where(news[s, q - 1] > 0.5, bounced, arrived)
            write(q, jnp.where(covered, ref[q], arrived))
        write(0, ref[0])
        refill = numerator / dens[s]
        replaced = uncovered & jnp.logical_not(covered)
        return refill, replaced, [jnp.where(covered, p, 0.0) for p in push]

    def refilled(refill, q):
        if q == 0:
            return refill * (WEIGHTS[0] * quiet)
        along = project(own_speed, q)
        return refill * (WEIGHTS[q] * (quiet + 3.0 * along + 4.5 * along * along))

    for copy in sends1:
        copy.wait_recv()

    def write_b(q, value):
        fine_b[q] = value

    refill, replaced, push1 = substep(0, halo1, fine_a, rho, write_b)
    for copy in sends1:
        copy.wait_send()

    def middle(q):
        return jnp.where(replaced, refilled(refill, q), fine_b[q])

    rho2 = collide(middle, write_a, FINE_RATE)
    halo2.pack(
        lambda q: rho2 if q == RHO + 100 else fine_a[q],
        fine_edges(fine_a, rho2),
        True,
        own_y,
        own_z,
        0,
    )
    sends2 = copies(halo2, 1)
    for copy in sends2:
        copy.start()

    for q in range(19):
        value = coarse[q]
        if q:
            value = halo1.pull(value, VELOCITIES[q], q, rows_c, lanes_c, 1)
        coarse_out[q] = value[:, 0:rows_c, 0:lanes_c]

    for copy in sends2:
        copy.wait_recv()

    def write_b2(q, value):
        fine_b[q] = value

    refill2, replaced2, push2 = substep(1, halo2, fine_a, rho2, write_b2)

    shape = force_own.shape[1:]
    row_at, lane_at = iota(shape, 0), iota(shape, 1)
    share = jnp.zeros(shape, jnp.float32)
    lane2 = iota((1, LANES), 1)
    for s, push in enumerate((push1, push2)):
        for d in range(3):
            column = jnp.sum(jnp.sum(push[d], axis=0), axis=0, keepdims=True)
            line = ((s * 3 + d) * box_x + bx0) * box_y + by0
            for i in range(local_z):
                within = (lane2 >= i * BOX_Z) & (lane2 < (i + 1) * BOX_Z)
                total = jnp.sum(jnp.where(within, column, 0.0), axis=1, keepdims=True)
                share = share + jnp.where((row_at == line) & (lane_at == bz0 + i), total, 0.0)

    reduced = []
    for axis, (buffer, sem) in enumerate(
        ((force_x, frecv_x), (force_y, frecv_y), (force_z, frecv_z))
    ):
        force_own[axis] = share
        sent = []
        for step in range(1, counts[axis]):
            c = tuple(step if a == axis else 0 for a in range(3))
            copy = pltpu.make_async_remote_copy(
                src_ref=force_own.at[axis],
                dst_ref=buffer.at[me[axis]],
                send_sem=fsend_sem.at[axis, step],
                recv_sem=sem.at[me[axis]],
                device_id=neighbour(c, counts, me),
                device_id_type=MESH,
            )
            copy.start()
            sent.append(copy)
        if axis == 0:
            for q in range(19):
                fine_out[q] = jnp.where(replaced2, refilled(refill2, q), fine_b[q])
        buffer[me[axis]] = share
        for step in range(1, counts[axis]):
            c = tuple(step if a == axis else 0 for a in range(3))
            source = neighbour(c, counts, me)
            pltpu.make_async_remote_copy(
                src_ref=force_own.at[axis],
                dst_ref=buffer.at[source[axis]],
                send_sem=fsend_sem.at[axis, step],
                recv_sem=sem.at[source[axis]],
                device_id=source,
                device_id_type=MESH,
            ).wait_recv()
        reduced += sent
        share = buffer[0]
        for i in range(1, counts[axis]):
            share = share + buffer[i]
    for s in range(2):
        for d in range(3):
            for bx in range(box_x):
                for by in range(box_y):
                    line = ((s * 3 + d) * box_x + bx) * box_y + by
                    force_out[s, d, bx, by : by + 1, :] = share[line : line + 1, 0:box_z]
    for copy in sends2 + reduced:
        copy.wait_send()


def shards(counts, coarse_pdfs, fine_pdfs, centers, sphere_velocity):
    own_x, own_y, own_z = fine_pdfs.shape[1:]
    assert (own_x, own_y, own_z) == (4, SUB, LANES)
    assert own_z % BOX_Z == 0 and BOX_XY % own_y == 0 and BOX_XY % own_x == 0
    boxes = centers.shape[2:]
    f32 = jnp.float32
    lines = -(-6 * boxes[0] * boxes[1] // SUB) * SUB

    def halo_scratch(x, y, z):
        return [
            pltpu.VMEM((2, x, SUB, LANES), f32),
            pltpu.VMEM((2, y, 1, LANES), f32),
            pltpu.VMEM((2, z, SUB, LANES), f32),
            pltpu.VMEM((2, x, SUB, LANES), f32),
            pltpu.VMEM((2, y, 1, LANES), f32),
            pltpu.VMEM((2, z, SUB, LANES), f32),
            pltpu.VMEM((4, FIRST_ROW, 1, LANES), f32),
            pltpu.VMEM((4, z, SUB, LANES), f32),
            pltpu.VMEM((4, z, SUB, LANES), f32),
        ]

    vmem = pl.BlockSpec(memory_space=pltpu.VMEM)
    smem = pl.BlockSpec(memory_space=pltpu.SMEM)
    return pl.pallas_call(
        functools.partial(kernel, counts),
        out_shape=(
            jax.ShapeDtypeStruct(coarse_pdfs.shape, f32),
            jax.ShapeDtypeStruct(fine_pdfs.shape, f32),
            jax.ShapeDtypeStruct((2, 3) + boxes, f32),
        ),
        in_specs=[vmem, vmem, smem, smem],
        out_specs=(vmem, vmem, vmem),
        scratch_shapes=[
            pltpu.VMEM((19, own_x, SUB, LANES), f32),
            pltpu.VMEM((19, own_x, SUB, LANES), f32),
            pltpu.VMEM((19, own_x, SUB, LANES), f32),
        ]
        + halo_scratch(11, ROWS, 2)
        + halo_scratch(6, COARSE_ROW, 1)
        + [
            pltpu.VMEM((2, 18, own_x, SUB, LANES), f32),
            pltpu.VMEM((2, 18, own_x, SUB, LANES), f32),
            pltpu.VMEM((3, own_x, SUB, LANES), f32),
            pltpu.VMEM((2, own_x, SUB, LANES), f32),
            pltpu.VMEM((12, SUB, LANES), f32),
            pltpu.VMEM((3, lines, LANES), f32),
            pltpu.VMEM((counts[0], lines, LANES), f32),
            pltpu.VMEM((counts[1], lines, LANES), f32),
            pltpu.VMEM((counts[2], lines, LANES), f32),
            pltpu.SemaphoreType.DMA((2, 18)),
            pltpu.SemaphoreType.DMA((2, 18)),
            pltpu.SemaphoreType.DMA((3, max(counts))),
            pltpu.SemaphoreType.DMA((counts[0],)),
            pltpu.SemaphoreType.DMA((counts[1],)),
            pltpu.SemaphoreType.DMA((counts[2],)),
        ],
        compiler_params=pltpu.CompilerParams(collective_id=0, has_side_effects=True),
    )(coarse_pdfs, fine_pdfs, centers, sphere_velocity)


def solution(mesh):
    counts = tuple(mesh.shape[a] for a in AXES)
    spec = P(None, "gx", "gy", "gz")
    return jax.shard_map(
        functools.partial(shards, counts),
        mesh=mesh,
        in_specs=(spec, spec, P(), P()),
        out_specs=(spec, spec, P()),
        check_vma=False,
    )
```

time: 145 us -> 30.7 us (0.21)
  blocking collectives: 36.8 us -> 0 us
  other arithmetic: 31.7 us -> 0 us
  local copies, waits for them, and re-layouts: 30.9 us -> 2.94 us
  Pallas kernels: 0 us -> 27 us
  starting transfers between devices: 20.7 us -> 0 us
  waiting for transfers between devices: 19.9 us -> 0 us
  matrix products: 2.62 us -> 0 us
    psum x1 -> x0, blocking collectives: 36.8 us -> none  [reduce_forces(): return lax.psum(forces, ('gx', 'gy', 'gz'))]
    pallas_call x0 -> x1, Pallas kernels: none -> 27 us  [shards(): pl.pallas_call(functools.partial(kernel, counts), out_shape=(jax.ShapeDty...]
    ppermute x18 -> x0, starting transfers between devices: 20.7 us -> none  [the longest x9 18.3 us: extended(): lax.ppermute(head, axis, [((i + 1) % count, i) for i in range(count)])]
    ppermute x18 -> x0, waiting for transfers between devices: 19.9 us -> none  [the longest x9 12.7 us: extended(): lax.ppermute(tail, axis, [(i, (i + 1) % count) for i in range(count)])]
    slice x19 -> x0, local copies, waits for them, and re-layouts: 15 us -> none  [the longest x2 3.83 us: with_explosion(): left_fill[:, trim_by:left_fill.shape[1] - trim_by, trim_by:left_fill.shap...]
    select_n x17 -> x0, other arithmetic: 9.64 us -> none  [the longest x2 3.81 us: with_explosion(): jnp.where(is_left, left_part[:, None], jnp.where(is_right, right_part[:,...]
    slice x4 -> x0, other arithmetic: 6.08 us -> none  [the longest x1 5.81 us: shards(): left_coal = coalesce(first_post[:, 1])]
    unnamed x72 -> x0, other arithmetic: 5.9 us -> none
  transfers between devices with their start and end apart: 18 -> 0, of which waited for: 10 -> 0; matrix products, arithmetic and copies ran while one was open for 21% -> 0% of each run, Pallas kernels for 0% -> 0%
where the time goes in v1:
time: 30.7 us; the launch traced here: 30.5 us
  Pallas kernels  27 us (88%)
  local copies, waits for them, and re-layouts  2.94 us (10%)
  between operations  0.65 us (2%)
    pallas_call x1, Pallas kernels, shards(): pl.pallas_call(functools.partial(kernel, counts), out_shape=(jax.ShapeDty...  27 us
    unnamed x7, local copies, waits for them, and re-layouts  2.94 us

profile of v1, /device:TPU:0, one launch (start us, length us, event | category | flops | bytes accessed | tf_op | source)
XLA Modules:
  0.0 30.5 jit_solution(12297969306411014212)
XLA Ops:
  0.6 27.0 %shard_map.67 = (f32[19,4,4,64]{3,2,1,0:T(4,128)}, f32[19,4,8,128]{3,2,1,0:T(8,128)}, f32[2,3,1,1,8]{4,3,2,1,0:T(1,128)}) custom-call(f32[19,4,4,64]{3,2,1,0:T(4,128)} %coarse_in.1, f32[19,4,8,128]{3,2,1,0:T(8,128)} %fine_in.1, s32[3,3,1,1,8]{4,3,2,1,0:T(1,128)} %centers.1, f32[3,1,1,8]{3,2,1,0:T(1,128)} %speeds.1), custom_call_target="tpu_custom_call" | custom-call | tf_op jit(solution)/shard_map/pallas_call | solution.py:646
  27.6 0.0 copy-start
  27.6 1.6 %copy.10 = f32[19,4,4,64]{3,2,1,0:T(4,128)} copy(f32[19,4,4,64]{3,2,1,0:T(4,128)} %get-tuple-element.6) | data formatting | bytes 155648
  29.2 0.0 copy-done
  29.2 0.0 copy-start.1
  29.2 0.7 %copy.11 = f32[19,4,8,128]{3,2,1,0:T(8,128)} copy(f32[19,4,8,128]{3,2,1,0:T(8,128)S(1)} %copy-done) | data formatting | bytes 622592
  30.0 0.0 copy-done.1
  30.0 0.6 %copy.12 = f32[2,3,1,1,8]{4,3,2,1,0:T(1,128)} copy(f32[2,3,1,1,8]{4,3,2,1,0:T(1,128)S(1)} %copy-done.1) | data formatting | bytes 384
Async XLA Ops:
  27.6 1.6 %copy-start = (f32[19,4,8,128]{3,2,1,0:T(8,128)S(1)}, f32[19,4,8,128]{3,2,1,0:T(8,128)}, u32[]{:S(2)}) copy-start(f32[19,4,8,128]{3,2,1,0:T(8,128)} %get-tuple-element.7) | copy-start | bytes 933892
  29.2 0.7 %copy-start.1 = (f32[2,3,1,1,8]{4,3,2,1,0:T(1,128)S(1)}, f32[2,3,1,1,8]{4,3,2,1,0:T(1,128)}, u32[]{:S(2)}) copy-start(f32[2,3,1,1,8]{4,3,2,1,0:T(1,128)} %get-tuple-element.8) | copy-start | bytes 580

commit v2 on v1

--- a/solution.py
+++ b/solution.py
@@ -53,6 +53,7 @@
 ROWS = 52
 LANES = 128
 SUB = 8
+VMEM_GRANT = 24 * 1024 * 1024
 
 
 def iota(shape, axis):
@@ -199,13 +200,20 @@
 
 def kernel(
     counts,
+    coarse_hbm,
+    fine_hbm,
+    centers_hbm,
+    speeds_hbm,
+    coarse_res,
+    fine_res,
+    force_res,
     coarse_in,
     fine_in,
     centers,
     speeds,
     coarse_out,
-    fine_out,
     force_out,
+    local_sem,
     fine_a,
     fine_b,
     coarse,
@@ -233,15 +241,9 @@
     dens,
     fill_ref,
     force_own,
-    force_x,
-    force_y,
-    force_z,
     send_sem,
     recv_sem,
-    fsend_sem,
-    frecv_x,
-    frecv_y,
-    frecv_z,
+    *force_parts,
 ):
     me = tuple(lax.axis_index(a) for a in AXES)
     own_x, own_y, own_z = fine_in.shape[1], fine_in.shape[2], fine_in.shape[3]
@@ -255,18 +257,33 @@
         pl.semaphore_signal(
             barrier, inc=1, device_id=neighbour(c, counts, me), device_id_type=MESH
         )
-    for axis in range(3):
-        for step in range(1, counts[axis]):
-            c = tuple(step if a == axis else 0 for a in range(3))
+    phases = force_phases(counts)
+    for phase in phases:
+        for c in group_steps(phase, counts):
             pl.semaphore_signal(
                 barrier, inc=1, device_id=neighbour(c, counts, me), device_id_type=MESH
             )
+    loads = [
+        pltpu.make_async_copy(src, dst, local_sem.at[i])
+        for i, (src, dst) in enumerate(
+            (
+                (fine_hbm, fine_in),
+                (coarse_hbm, coarse_in),
+                (centers_hbm, centers),
+                (speeds_hbm, speeds),
+            )
+        )
+    ]
+    for copy in loads:
+        copy.start()
+    loads[0].wait()
 
     def write_a(q, value):
         fine_a[q] = value
 
     rho = collide(lambda q: fine_in[q], write_a, FINE_RATE)
     coarse[...] = jnp.ones(coarse.shape, jnp.float32)
+    loads[1].wait()
     coarse[:, :, 0:rows_c, 0:lanes_c] = coarse_in[...]
 
     def write_c(q, value):
@@ -380,12 +397,14 @@
             )
         return made
 
-    pl.semaphore_wait(barrier, 18 + sum(n - 1 for n in counts))
+    pl.semaphore_wait(barrier, 18 + sum(len(group_steps(p, counts)) for p in phases))
     sends1 = copies(halo1, 0)
     for copy in sends1:
         copy.start()
 
-    start_x, start_y, start_z = me[0] * own_x, me[1] * own_y, me[2] * own_z
+    loads[2].wait()
+    loads[3].wait()
+    start_x, start_y = me[0] * own_x, me[1] * own_y
     total_y = own_y * counts[1]
     bx0 = lax.div(start_x, BOX_XY)
     by0 = lax.div(start_y, BOX_XY)
@@ -551,6 +570,8 @@
         if q:
             value = halo1.pull(value, VELOCITIES[q], q, rows_c, lanes_c, 1)
         coarse_out[q] = value[:, 0:rows_c, 0:lanes_c]
+    stores = [pltpu.make_async_copy(coarse_out, coarse_res, local_sem.at[4])]
+    stores[0].start()
 
     for copy in sends2:
         copy.wait_recv()
@@ -561,7 +582,7 @@
     refill2, replaced2, push2 = substep(1, halo2, fine_a, rho2, write_b2)
 
     shape = force_own.shape[1:]
-    row_at, lane_at = iota(shape, 0), iota(shape, 1)
+    flat_at = iota(shape, 0) * LANES + iota(shape, 1)
     share = jnp.zeros(shape, jnp.float32)
     lane2 = iota((1, LANES), 1)
     for s, push in enumerate((push1, push2)):
@@ -571,53 +592,86 @@
             for i in range(local_z):
                 within = (lane2 >= i * BOX_Z) & (lane2 < (i + 1) * BOX_Z)
                 total = jnp.sum(jnp.where(within, column, 0.0), axis=1, keepdims=True)
-                share = share + jnp.where((row_at == line) & (lane_at == bz0 + i), total, 0.0)
+                share = share + jnp.where(flat_at == line * box_z + bz0 + i, total, 0.0)
 
     reduced = []
-    for axis, (buffer, sem) in enumerate(
-        ((force_x, frecv_x), (force_y, frecv_y), (force_z, frecv_z))
-    ):
-        force_own[axis] = share
-        sent = []
-        for step in range(1, counts[axis]):
-            c = tuple(step if a == axis else 0 for a in range(3))
+    for number, phase in enumerate(phases):
+        buffer, out_sem, in_sem = force_parts[3 * number : 3 * number + 3]
+        steps = group_steps(phase, counts)
+        rank = group_rank(phase, counts, me)
+        force_own[number] = share
+        for i, c in enumerate(steps):
             copy = pltpu.make_async_remote_copy(
-                src_ref=force_own.at[axis],
-                dst_ref=buffer.at[me[axis]],
-                send_sem=fsend_sem.at[axis, step],
-                recv_sem=sem.at[me[axis]],
+                src_ref=force_own.at[number],
+                dst_ref=buffer.at[rank],
+                send_sem=out_sem.at[i],
+                recv_sem=in_sem.at[rank],
                 device_id=neighbour(c, counts, me),
                 device_id_type=MESH,
             )
             copy.start()
-            sent.append(copy)
-        if axis == 0:
+            reduced.append(copy)
+        if number == 0:
             for q in range(19):
-                fine_out[q] = jnp.where(replaced2, refilled(refill2, q), fine_b[q])
-        buffer[me[axis]] = share
-        for step in range(1, counts[axis]):
-            c = tuple(step if a == axis else 0 for a in range(3))
+                fine_b[q] = jnp.where(replaced2, refilled(refill2, q), fine_b[q])
+            stores.append(pltpu.make_async_copy(fine_b, fine_res, local_sem.at[5]))
+            stores[1].start()
+        buffer[rank] = share
+        for i, c in enumerate(steps):
             source = neighbour(c, counts, me)
+            at = group_rank(phase, counts, source)
             pltpu.make_async_remote_copy(
-                src_ref=force_own.at[axis],
-                dst_ref=buffer.at[source[axis]],
-                send_sem=fsend_sem.at[axis, step],
-                recv_sem=sem.at[source[axis]],
+                src_ref=force_own.at[number],
+                dst_ref=buffer.at[at],
+                send_sem=out_sem.at[i],
+                recv_sem=in_sem.at[at],
                 device_id=source,
                 device_id_type=MESH,
             ).wait_recv()
-        reduced += sent
-        share = buffer[0]
-        for i in range(1, counts[axis]):
-            share = share + buffer[i]
+        share = jnp.sum(buffer[...], axis=0)
     for s in range(2):
         for d in range(3):
             for bx in range(box_x):
                 for by in range(box_y):
-                    line = ((s * 3 + d) * box_x + bx) * box_y + by
-                    force_out[s, d, bx, by : by + 1, :] = share[line : line + 1, 0:box_z]
+                    first_at = (((s * 3 + d) * box_x + bx) * box_y + by) * box_z
+                    moved = pltpu.roll(share, -first_at % LANES, 1)
+                    line = first_at // LANES
+                    force_out[s, d, bx, by : by + 1, :] = moved[line : line + 1, 0:box_z]
+    stores.append(pltpu.make_async_copy(force_out, force_res, local_sem.at[6]))
+    stores[2].start()
     for copy in sends2 + reduced:
         copy.wait_send()
+    for copy in stores:
+        copy.wait()
+
+
+def force_phases(counts):
+    if counts[0] * counts[1] * counts[2] <= 64:
+        return ((0, 1, 2),)
+    return ((0,), (1,), (2,))
+
+
+def group_steps(phase, counts):
+    spans = [range(counts[a]) if a in phase else range(1) for a in range(3)]
+    steps = [(x, y, z) for x in spans[0] for y in spans[1] for z in spans[2]]
+    return steps[1:]
+
+
+def group_rank(phase, counts, at):
+    rank = 0
+    for a in phase:
+        rank = rank * counts[a] + at[a]
+    return rank
+
+
+def finish(*refs):
+    n = len(refs) // 2
+    sem = refs[2 * n]
+    outs = [pltpu.make_async_copy(refs[i], refs[n + i], sem.at[i]) for i in range(n)]
+    for copy in outs:
+        copy.start()
+    for copy in outs:
+        copy.wait()
 
 
 def shards(counts, coarse_pdfs, fine_pdfs, centers, sphere_velocity):
@@ -626,7 +680,18 @@
     assert own_z % BOX_Z == 0 and BOX_XY % own_y == 0 and BOX_XY % own_x == 0
     boxes = centers.shape[2:]
     f32 = jnp.float32
-    lines = -(-6 * boxes[0] * boxes[1] // SUB) * SUB
+    lines = -(-6 * boxes[0] * boxes[1] * boxes[2] // LANES)
+    lines = lines if lines == 1 else -(-lines // SUB) * SUB
+    assert LANES % boxes[2] == 0
+    phases = force_phases(counts)
+    force_scratch = []
+    for phase in phases:
+        size = len(group_steps(phase, counts)) + 1
+        force_scratch += [
+            pltpu.VMEM((size, lines, LANES), f32),
+            pltpu.SemaphoreType.DMA((size - 1,)),
+            pltpu.SemaphoreType.DMA((size,)),
+        ]
 
     def halo_scratch(x, y, z):
         return [
@@ -641,18 +706,25 @@
             pltpu.VMEM((4, z, SUB, LANES), f32),
         ]
 
-    vmem = pl.BlockSpec(memory_space=pltpu.VMEM)
-    smem = pl.BlockSpec(memory_space=pltpu.SMEM)
-    return pl.pallas_call(
+    anywhere = pl.BlockSpec(memory_space=pl.ANY)
+    out_shape = (
+        jax.ShapeDtypeStruct(coarse_pdfs.shape, f32),
+        jax.ShapeDtypeStruct(fine_pdfs.shape, f32),
+        jax.ShapeDtypeStruct((2, 3) + boxes, f32),
+    )
+    results = pl.pallas_call(
         functools.partial(kernel, counts),
-        out_shape=(
-            jax.ShapeDtypeStruct(coarse_pdfs.shape, f32),
-            jax.ShapeDtypeStruct(fine_pdfs.shape, f32),
-            jax.ShapeDtypeStruct((2, 3) + boxes, f32),
-        ),
-        in_specs=[vmem, vmem, smem, smem],
-        out_specs=(vmem, vmem, vmem),
+        out_shape=out_shape,
+        in_specs=[pl.BlockSpec(memory_space=pltpu.HBM)] * 4,
+        out_specs=(anywhere,) * 3,
         scratch_shapes=[
+            pltpu.VMEM(coarse_pdfs.shape, f32),
+            pltpu.VMEM(fine_pdfs.shape, f32),
+            pltpu.SMEM(centers.shape, jnp.int32),
+            pltpu.SMEM(sphere_velocity.shape, f32),
+            pltpu.VMEM(coarse_pdfs.shape, f32),
+            pltpu.VMEM((2, 3) + boxes, f32),
+            pltpu.SemaphoreType.DMA((7,)),
             pltpu.VMEM((19, own_x, SUB, LANES), f32),
             pltpu.VMEM((19, own_x, SUB, LANES), f32),
             pltpu.VMEM((19, own_x, SUB, LANES), f32),
@@ -665,19 +737,23 @@
             pltpu.VMEM((3, own_x, SUB, LANES), f32),
             pltpu.VMEM((2, own_x, SUB, LANES), f32),
             pltpu.VMEM((12, SUB, LANES), f32),
-            pltpu.VMEM((3, lines, LANES), f32),
-            pltpu.VMEM((counts[0], lines, LANES), f32),
-            pltpu.VMEM((counts[1], lines, LANES), f32),
-            pltpu.VMEM((counts[2], lines, LANES), f32),
+            pltpu.VMEM((len(phases), lines, LANES), f32),
             pltpu.SemaphoreType.DMA((2, 18)),
             pltpu.SemaphoreType.DMA((2, 18)),
-            pltpu.SemaphoreType.DMA((3, max(counts))),
-            pltpu.SemaphoreType.DMA((counts[0],)),
-            pltpu.SemaphoreType.DMA((counts[1],)),
-            pltpu.SemaphoreType.DMA((counts[2],)),
-        ],
-        compiler_params=pltpu.CompilerParams(collective_id=0, has_side_effects=True),
+        ]
+        + force_scratch,
+        compiler_params=pltpu.CompilerParams(
+            collective_id=0, has_side_effects=True, vmem_limit_bytes=VMEM_GRANT
+        ),
     )(coarse_pdfs, fine_pdfs, centers, sphere_velocity)
+    return pl.pallas_call(
+        finish,
+        out_shape=out_shape,
+        in_specs=[anywhere] * 3,
+        out_specs=(anywhere,) * 3,
+        scratch_shapes=[pltpu.SemaphoreType.DMA((3,))],
+        compiler_params=pltpu.CompilerParams(vmem_limit_bytes=VMEM_GRANT),
+    )(*results)
 
 
 def solution(mesh):

time: 30.7 us -> 26.7 us (0.87)
  Pallas kernels: 27 us -> 22.6 us
    pallas_call x1 -> x2, Pallas kernels: 27 us -> 22.6 us  [the longest x1 21.8 us: shards(): pl.pallas_call(functools.partial(kernel, counts), out_shape=out_shape, in...]
    unnamed x7 -> x8, local copies, waits for them, and re-layouts: 2.94 us -> 3.24 us
where the time goes in v2:
time: 26.7 us; the launch traced here: 26.5 us
  Pallas kernels  22.6 us (85%)
  local copies, waits for them, and re-layouts  3.24 us (12%)
  between operations  0.65 us (2%)
    pallas_call x1, Pallas kernels, shards(): pl.pallas_call(functools.partial(kernel, counts), out_shape=out_shape, in...  21.8 us
    unnamed x8, local copies, waits for them, and re-layouts  3.24 us
    pallas_call x1, Pallas kernels, shards(): pl.pallas_call(finish, out_shape=out_shape, in_specs=[anywhere] * 3, out_...  0.8 us

profile of v2, /device:TPU:0, one launch (start us, length us, event | category | flops | bytes accessed | tf_op | source)
XLA Modules:
  0.0 26.5 jit_solution(12503796819103661289)
XLA Ops:
  0.6 0.0 copy-start
  0.6 1.0 %copy-done = f32[19,4,8,128]{3,2,1,0:T(8,128)S(1)} copy-done((f32[19,4,8,128]{3,2,1,0:T(8,128)S(1)}, f32[19,4,8,128]{3,2,1,0:T(8,128)}, u32[]{:S(2)}) %copy-start) | copy-done | bytes 311320
  1.6 0.0 copy-start.1
  1.6 0.9 %copy-done.1 = f32[19,4,4,64]{3,2,1,0:T(4,128)S(1)} copy-done((f32[19,4,4,64]{3,2,1,0:T(4,128)S(1)}, f32[19,4,4,64]{3,2,1,0:T(4,128)}, u32[]{:S(2)}) %copy-start.1) | copy-done | bytes 77848
  2.5 0.0 copy-start.2
  2.5 0.7 %copy-done.2 = s32[3,3,1,1,8]{4,3,2,1,0:T(1,128)S(1)} copy-done((s32[3,3,1,1,8]{4,3,2,1,0:T(1,128)S(1)}, s32[3,3,1,1,8]{4,3,2,1,0:T(1,128)}, u32[]{:S(2)}) %copy-start.2) | copy-done | bytes 312
  3.2 0.0 copy-start.3
  3.2 0.7 %copy-done.3 = f32[3,1,1,8]{3,2,1,0:T(1,128)S(1)} copy-done((f32[3,1,1,8]{3,2,1,0:T(1,128)S(1)}, f32[3,1,1,8]{3,2,1,0:T(1,128)}, u32[]{:S(2)}) %copy-start.3) | copy-done | bytes 120
  3.9 21.8 %shard_map.67 = (f32[19,4,4,64]{3,2,1,0:T(4,128)S(1)}, f32[19,4,8,128]{3,2,1,0:T(8,128)S(1)}, f32[2,3,1,1,8]{4,3,2,1,0:T(1,128)S(1)}) custom-call(f32[19,4,4,64]{3,2,1,0:T(4,128)S(1)} %copy-done.1, f32[19,4,8,128]{3,2,1,0:T(8,128)S(1)} %copy-done, s32[3,3,1,1,8]{4,3,2,1,0:T(1,128)S(1)} %copy-done.2, f32[3,1,1,8]{3,2,1,0:T(1,128)S(1)} %copy-done.3), custom_call_target="tpu_custom_call" | custom-call | tf_op jit(solution)/shard_map/pallas_call | solution.py:715
  25.7 0.8 %shard_map.68 = (f32[19,4,4,64]{3,2,1,0:T(4,128)}, f32[19,4,8,128]{3,2,1,0:T(8,128)}, f32[2,3,1,1,8]{4,3,2,1,0:T(1,128)}) custom-call(f32[19,4,4,64]{3,2,1,0:T(4,128)S(1)} %get-tuple-element.6.refs_0_, f32[19,4,8,128]{3,2,1,0:T(8,128)S(1)} %get-tuple-element.7.refs_1_, f32[2,3,1,1,8]{4,3,2,1,0:T(1,128)S(1)} %get-tuple-element.8.refs_2_), custom_call_target="tpu_custom_call" | custom-call | tf_op jit(solution)/shard_map/pallas_call | solution.py:749
Async XLA Ops:
  0.6 1.0 %copy-start = (f32[19,4,8,128]{3,2,1,0:T(8,128)S(1)}, f32[19,4,8,128]{3,2,1,0:T(8,128)}, u32[]{:S(2)}) copy-start(f32[19,4,8,128]{3,2,1,0:T(8,128)} %fine_hbm.1) | copy-start | bytes 933892
  1.6 0.9 %copy-start.1 = (f32[19,4,4,64]{3,2,1,0:T(4,128)S(1)}, f32[19,4,4,64]{3,2,1,0:T(4,128)}, u32[]{:S(2)}) copy-start(f32[19,4,4,64]{3,2,1,0:T(4,128)} %coarse_hbm.1) | copy-start | bytes 233476
  2.5 0.7 %copy-start.2 = (s32[3,3,1,1,8]{4,3,2,1,0:T(1,128)S(1)}, s32[3,3,1,1,8]{4,3,2,1,0:T(1,128)}, u32[]{:S(2)}) copy-start(s32[3,3,1,1,8]{4,3,2,1,0:T(1,128)} %centers_hbm.1) | copy-start | bytes 868
  3.2 0.7 %copy-start.3 = (f32[3,1,1,8]{3,2,1,0:T(1,128)S(1)}, f32[3,1,1,8]{3,2,1,0:T(1,128)}, u32[]{:S(2)}) copy-start(f32[3,1,1,8]{3,2,1,0:T(1,128)} %speeds_hbm.1) | copy-start | bytes 292

commit v3 on v2

--- a/solution.py
+++ b/solution.py
@@ -306,6 +306,75 @@
         tall = jnp.where(row3 < 2 * r + 2, wide[:, r : r + 1, :], tall)
     fill_ref[...] = tall
 
+    def fine_edges(ref, density):
+        def plane(sign):
+            ix, at_end, base = (3, last, 0) if sign == 1 else (0, first, 6)
+
+            def get(q):
+                is_rho = q == RHO + 100
+                k = RHO if is_rho else MOVERS[0, sign].index(q)
+                mine = density[ix] if is_rho else ref[q, ix]
+                return jnp.where(at_end, fill_ref[base + k], mine)
+
+            return get
+
+        return {1: plane(1), -1: plane(-1)}
+
+    halo1 = Halo((sx1, sy1, sz1), (rx1, ry1, rz1, rxy1, rxz1, ryz1))
+    halo2 = Halo((sx2, sy2, sz2), (rx2, ry2, rz2, rxy2, rxz2, ryz2))
+    halo1.pack(
+        lambda q: rho if q == RHO + 100 else fine_a[q],
+        fine_edges(fine_a, rho),
+        True,
+        own_y,
+        own_z,
+        0,
+    )
+    def copies(halo, phase):
+        coarse_part = phase == 2
+        x_part = pl.ds(6, 5) if coarse_part else pl.ds(0, 6)
+        y_first, y_last = (COARSE_ROW, ROWS) if coarse_part else (FIRST_ROW, COARSE_ROW)
+        y_part = pl.ds(y_first, y_last - y_first)
+        edge_part = pl.ds(4, 4) if coarse_part else pl.ds(0, 4)
+        z_part = 1 if coarse_part else 0
+        made = []
+        for i, c in enumerate(DIRS):
+            cx, cy, cz = c
+            if cz:
+                if cx:
+                    dst = halo.rxz.at[PAIR_SLOT[cx, cz], z_part]
+                elif cy:
+                    dst = halo.ryz.at[PAIR_SLOT[cy, cz], z_part]
+                else:
+                    dst = halo.rz.at[SLOT[cz], z_part]
+                src = halo.sz.at[SLOT[cz], z_part]
+            elif cy:
+                if cx:
+                    src = halo.sy.at[SLOT[cy], edge_part]
+                    dst = halo.rxy.at[PAIR_SLOT[cx, cy], edge_part]
+                else:
+                    src = halo.sy.at[SLOT[cy], y_part]
+                    dst = halo.ry.at[SLOT[cy], y_part]
+            else:
+                src = halo.sx.at[SLOT[cx], x_part]
+                dst = halo.rx.at[SLOT[cx], x_part]
+            made.append(
+                pltpu.make_async_remote_copy(
+                    src_ref=src,
+                    dst_ref=dst,
+                    send_sem=send_sem.at[phase, i],
+                    recv_sem=recv_sem.at[phase, i],
+                    device_id=neighbour(c, counts, me),
+                    device_id_type=MESH,
+                )
+            )
+        return made
+
+    pl.semaphore_wait(barrier, 18 + sum(len(group_steps(p, counts)) for p in phases))
+    sends1 = copies(halo1, 0)
+    for copy in reversed(sends1):
+        copy.start()
+
     planes = []
     for sign, ix in ((1, 3), (-1, 0)):
         for q in MOVERS[0, sign]:
@@ -322,20 +391,6 @@
     for r in (2, 1, 0):
         flat = jnp.where(row3 <= r, thin[:, 2 * r : 2 * r + 1, :], flat)
 
-    def fine_edges(ref, density):
-        def plane(sign):
-            ix, at_end, base = (3, last, 0) if sign == 1 else (0, first, 6)
-
-            def get(q):
-                is_rho = q == RHO + 100
-                k = RHO if is_rho else MOVERS[0, sign].index(q)
-                mine = density[ix] if is_rho else ref[q, ix]
-                return jnp.where(at_end, fill_ref[base + k], mine)
-
-            return get
-
-        return {1: plane(1), -1: plane(-1)}
-
     def coarse_edge(sign):
         ix, at_end, base = (3, last, 0) if sign == 1 else (0, first, 5)
 
@@ -344,16 +399,6 @@
 
         return get
 
-    halo1 = Halo((sx1, sy1, sz1), (rx1, ry1, rz1, rxy1, rxz1, ryz1))
-    halo2 = Halo((sx2, sy2, sz2), (rx2, ry2, rz2, rxy2, rxz2, ryz2))
-    halo1.pack(
-        lambda q: rho if q == RHO + 100 else fine_a[q],
-        fine_edges(fine_a, rho),
-        True,
-        own_y,
-        own_z,
-        0,
-    )
     halo1.pack(
         lambda q: coarse[q],
         {1: coarse_edge(1), -1: coarse_edge(-1)},
@@ -363,43 +408,8 @@
         1,
     )
 
-    def copies(halo, phase):
-        made = []
-        for i, c in enumerate(DIRS):
-            cx, cy, cz = c
-            if cz:
-                if cx:
-                    dst = halo.rxz.at[PAIR_SLOT[cx, cz]]
-                elif cy:
-                    dst = halo.ryz.at[PAIR_SLOT[cy, cz]]
-                else:
-                    dst = halo.rz.at[SLOT[cz]]
-                src = halo.sz.at[SLOT[cz]]
-            elif cy:
-                if cx:
-                    src = halo.sy.at[SLOT[cy], pl.ds(0, FIRST_ROW)]
-                    dst = halo.rxy.at[PAIR_SLOT[cx, cy]]
-                else:
-                    src = halo.sy.at[SLOT[cy]]
-                    dst = halo.ry.at[SLOT[cy]]
-            else:
-                src = halo.sx.at[SLOT[cx]]
-                dst = halo.rx.at[SLOT[cx]]
-            made.append(
-                pltpu.make_async_remote_copy(
-                    src_ref=src,
-                    dst_ref=dst,
-                    send_sem=send_sem.at[phase, i],
-                    recv_sem=recv_sem.at[phase, i],
-                    device_id=neighbour(c, counts, me),
-                    device_id_type=MESH,
-                )
-            )
-        return made
-
-    pl.semaphore_wait(barrier, 18 + sum(len(group_steps(p, counts)) for p in phases))
-    sends1 = copies(halo1, 0)
-    for copy in sends1:
+    sends_c = copies(halo1, 2)
+    for copy in reversed(sends_c):
         copy.start()
 
     loads[2].wait()
@@ -562,9 +572,11 @@
         0,
     )
     sends2 = copies(halo2, 1)
-    for copy in sends2:
+    for copy in reversed(sends2):
         copy.start()
 
+    for copy in sends_c:
+        copy.wait_recv()
     for q in range(19):
         value = coarse[q]
         if q:
@@ -639,7 +651,7 @@
                     force_out[s, d, bx, by : by + 1, :] = moved[line : line + 1, 0:box_z]
     stores.append(pltpu.make_async_copy(force_out, force_res, local_sem.at[6]))
     stores[2].start()
-    for copy in sends2 + reduced:
+    for copy in sends_c + sends2 + reduced:
         copy.wait_send()
     for copy in stores:
         copy.wait()
@@ -738,14 +750,19 @@
             pltpu.VMEM((2, own_x, SUB, LANES), f32),
             pltpu.VMEM((12, SUB, LANES), f32),
             pltpu.VMEM((len(phases), lines, LANES), f32),
-            pltpu.SemaphoreType.DMA((2, 18)),
-            pltpu.SemaphoreType.DMA((2, 18)),
+            pltpu.SemaphoreType.DMA((3, 18)),
+            pltpu.SemaphoreType.DMA((3, 18)),
         ]
         + force_scratch,
         compiler_params=pltpu.CompilerParams(
             collective_id=0, has_side_effects=True, vmem_limit_bytes=VMEM_GRANT
         ),
-    )(coarse_pdfs, fine_pdfs, centers, sphere_velocity)
+    )(
+        *[
+            pltpu.with_memory_space_constraint(x, pltpu.HBM)
+            for x in (coarse_pdfs, fine_pdfs, centers, sphere_velocity)
+        ]
+    )
     return pl.pallas_call(
         finish,
         out_shape=out_shape,

time: 26.7 us -> 23.3 us (0.87)
  local copies, waits for them, and re-layouts: 3.24 us -> 0 us
    unnamed x8 -> x0, local copies, waits for them, and re-layouts: 3.24 us -> none
where the time goes in v3:
time: 23.3 us; the launch traced here: 23.1 us
  Pallas kernels  22.5 us (97%)
  between operations  0.64 us (3%)
    pallas_call x1, Pallas kernels, shards(): pl.pallas_call(functools.partial(kernel, counts), out_shape=out_shape, in...  21.7 us
    pallas_call x1, Pallas kernels, shards(): pl.pallas_call(finish, out_shape=out_shape, in_specs=[anywhere] * 3, out_...  0.8 us

profile of v3, /device:TPU:0, one launch (start us, length us, event | category | flops | bytes accessed | tf_op | source)
XLA Modules:
  0.0 23.1 jit_solution(2811355470577640443)
XLA Ops:
  0.6 21.7 %shard_map.67 = (f32[19,4,4,64]{3,2,1,0:T(4,128)S(1)}, f32[19,4,8,128]{3,2,1,0:T(8,128)S(1)}, f32[2,3,1,1,8]{4,3,2,1,0:T(1,128)S(1)}) custom-call(f32[19,4,4,64]{3,2,1,0:T(4,128)} %coarse_hbm.1, f32[19,4,8,128]{3,2,1,0:T(8,128)} %fine_hbm.1, s32[3,3,1,1,8]{4,3,2,1,0:T(1,128)} %centers_hbm.1, f32[3,1,1,8]{3,2,1,0:T(1,128)} %speeds_hbm.1), custom_call_target="tpu_custom_call" | custom-call | tf_op jit(solution)/shard_map/pallas_call | solution.py:727
  22.3 0.8 %shard_map.68 = (f32[19,4,4,64]{3,2,1,0:T(4,128)}, f32[19,4,8,128]{3,2,1,0:T(8,128)}, f32[2,3,1,1,8]{4,3,2,1,0:T(1,128)}) custom-call(f32[19,4,4,64]{3,2,1,0:T(4,128)S(1)} %get-tuple-element.6.refs_0_, f32[19,4,8,128]{3,2,1,0:T(8,128)S(1)} %get-tuple-element.7.refs_1_, f32[2,3,1,1,8]{4,3,2,1,0:T(1,128)S(1)} %get-tuple-element.8.refs_2_), custom_call_target="tpu_custom_call" | custom-call | tf_op jit(solution)/shard_map/pallas_call | solution.py:766
